TPU v7x, 128 devices: a whole 4x4x4 slice. The times are simulated.
128 devices in a mesh: bead: 16 (over x, y_hi, core), atom: 8 (over z, y_lo).
Axes of the slice: x: 4, y: 4 (y_hi: 2, y_lo: 2; y = y_hi * 2 + y_lo), z: 4, core: 2. Of those that a mesh axis runs over, the one named last changes fastest.
Arguments:
- replica_point_fractions: float32 [128, 3, 12288], P('bead', None, 'atom'), may hold values from -1 to 2, as said below
- inverse_lattice_integers: int32 [3, 2048], P(None, 'bead'), may hold values from -10 to 10, as said below
- point_species_labels: int32 [12288], P('atom'), may hold values from 0 to 3
- species_electric_values: float32 [4], replicated, may hold values from -1 to 1
Outputs:
- bead_forces: float32 [128, 3, 12288], P('bead', None, 'atom')
Inputs may be any that keep to these rules, and one draw needn't show every extreme that they name: replica_point_fractions holds a site's position near a common centre in all beads, with its own offset in each bead. `inverse_lattice_integers`: its columns are distinct, none is all zeros, and none is the negative of another (the first nonzero entry of each column is positive).
All inputs are finite; a program needn't handle non-finite values.
Results may differ from a plain program's by a relative error of at most 0.0003.
Values sent between devices are 32-bit elements; how exact they have to be, the bound alone decides.
No kernel may reach another device: no remote copies, remote signals or barrier semaphores. Data moves between devices by JAX's collectives and lax.ppermute only.
A program may use at most 64 MiB of HBM per device.

v0:
```python
import math

import jax
import jax.numpy as jnp
from jax import lax
from jax.sharding import PartitionSpec as P

CONTR = 8


TWO_PI = 2.0 * math.pi


def copy_for_each(array, axis):
    peers = lax.axis_size(axis)
    return lax.all_to_all(
        jnp.broadcast_to(array[None], (peers, *array.shape)), axis, 0, 0, tiled=True
    )


def over_copies(array, axis):
    return copy_for_each(array, axis).sum(axis=0)


def packed_total(arrays, axis):
    ends = [0]
    for a in arrays:
        ends.append(ends[-1] + a.size)
    total = over_copies(jnp.concatenate([a.ravel() for a in arrays]), axis)
    return tuple((total[b:e].reshape(a.shape) for a, b, e in zip(arrays, ends, ends[1:])))


def in_blocks(array, dim, peers):
    before, after = (array.shape[:dim], array.shape[dim + 1 :])
    return jnp.moveaxis(array.reshape(*before, peers, -1, *after), dim, 0)


def summed_on_arrival(array, axis, dim):
    peers = lax.axis_size(axis)
    blocks = lax.all_to_all(in_blocks(array, dim, peers), axis, 0, 0, tiled=True)
    return jnp.sum(blocks, axis=0)


def cycle_modes(length, count):
    index = jnp.arange(length, dtype=jnp.float32)
    rows = [jnp.ones((length,), jnp.float32) / math.sqrt(length)]
    for mode in range(1, count // 2):
        rows.append(math.sqrt(2.0 / length) * jnp.cos(TWO_PI * mode * index / length))
        rows.append(math.sqrt(2.0 / length) * jnp.sin(TWO_PI * mode * index / length))
    if length == count:
        rows.append(jnp.cos(math.pi * index) / math.sqrt(length))
    else:
        rows.append(math.sqrt(2.0 / length) * jnp.cos(TWO_PI * (count // 2) * index / length))
    return jnp.stack(rows)


def contraction_table(beads, contr):
    small = cycle_modes(contr, contr)
    big = cycle_modes(beads, contr)
    return math.sqrt(contr / beads) * jnp.dot(small.T, big, precision=lax.Precision.HIGHEST)


def fourier_mode_scaling(inverse_lattice_integers, number_points):
    fourier_mode_table = inverse_lattice_integers.astype(jnp.float32)
    square = jnp.sum(fourier_mode_table * fourier_mode_table, axis=0)
    return (fourier_mode_table, 4.0 * jnp.exp(-square / 100.0) / (square * number_points))


def phases(fourier_mode_table, position):
    return TWO_PI * jnp.dot(fourier_mode_table.T, position, precision=lax.Precision.HIGHEST)


def factor_parts(fourier_mode_table, charge, contracted):

    def structure(position):
        angle = phases(fourier_mode_table, position)
        return (
            jnp.dot(jnp.cos(angle), charge, precision=lax.Precision.HIGHEST),
            jnp.dot(jnp.sin(angle), charge, precision=lax.Precision.HIGHEST),
        )

    return lax.map(structure, contracted)


def force_parts(fourier_mode_table, fourier_mode_factor, charge, contracted, cos_fac, sin_fac):

    def forces(items):
        position, cfac, sfac = items
        angle = phases(fourier_mode_table, position)
        left = TWO_PI * fourier_mode_table * (fourier_mode_factor * cfac)[None, :]
        right = TWO_PI * fourier_mode_table * (fourier_mode_factor * sfac)[None, :]
        term = jnp.dot(left, jnp.sin(angle), precision=lax.Precision.HIGHEST) - jnp.dot(
            right, jnp.cos(angle), precision=lax.Precision.HIGHEST
        )
        return charge[None, :] * term

    return lax.map(forces, (contracted, cos_fac, sin_fac))


def local(
    replica_point_fractions, inverse_lattice_integers, point_species_labels, species_electric_values
):
    beads_local = replica_point_fractions.shape[0]
    beads = beads_local * lax.axis_size("bead")
    table = contraction_table(beads, CONTR)
    first_bead = lax.axis_index("bead") * beads_local
    local_table = lax.dynamic_slice_in_dim(table, first_bead, beads_local, 1)
    kinds = jnp.arange(species_electric_values.shape[0], dtype=jnp.int32)
    charge = jnp.sum(
        (point_species_labels[None, :] == kinds[:, None]).astype(jnp.float32)
        * species_electric_values[:, None],
        axis=0,
    )
    number_points = point_species_labels.shape[0] * lax.axis_size("atom")
    portion = jnp.einsum(
        "jb,bxs->jxs", local_table, replica_point_fractions, precision=lax.Precision.HIGHEST
    )
    contracted = over_copies(portion, "bead")
    fourier_mode_table, fourier_mode_factor = fourier_mode_scaling(
        inverse_lattice_integers, number_points
    )
    cos_part, sin_part = factor_parts(fourier_mode_table, charge, contracted)
    cos_fac, sin_fac = packed_total((cos_part, sin_part), "atom")
    partial_force = force_parts(
        fourier_mode_table, fourier_mode_factor, charge, contracted, cos_fac, sin_fac
    )
    share = summed_on_arrival(partial_force, "bead", 2)
    expanded = jnp.einsum("jb,jxs->bxs", table, share, precision=lax.Precision.HIGHEST)
    return lax.all_to_all(expanded, "bead", split_axis=0, concat_axis=2, tiled=True)


def solution(mesh):
    in_specs = (P("bead", None, "atom"), P(None, "bead"), P("atom"), P())
    out_specs = P("bead", None, "atom")
    return jax.shard_map(local, mesh=mesh, in_specs=in_specs, out_specs=out_specs, check_vma=False)
```

profile of v0, /device:TPU:1, one launch (start us, length us, event | category | flops | bytes accessed | tf_op | source)
XLA Modules:
  0.0 219.6 jit_solution(4924902976064297701)
XLA Ops:
  0.9 0.3 fusion.27
  1.3 1.7 broadcast_in_dim.17
  3.0 8.6 %all-to-all-start = ((f32[16,8,3,1536]{3,1,2,0:T(8,128)}), f32[16,8,3,1536]{3,1,2,0:T(8,128)S(1)}, u32[]{:S(2)}, u32[]{:S(2)}) async-start(f32[16,8,3,1536]{3,1,2,0:T(8,128)} %broadcast_in_dim.17), calls=%async_computation | async-start | bytes 4718592 | tf_op jit(solution)/shard_map/all_to_all | solution.py:16
  11.7 30.9 %all-to-all-done = f32[16,8,3,1536]{3,1,2,0:T(8,128)S(1)} async-done(((f32[16,8,3,1536]{3,1,2,0:T(8,128)}), f32[16,8,3,1536]{3,1,2,0:T(8,128)S(1)}, u32[]{:S(2)}, u32[]{:S(2)}) %all-to-all-start) | async-done | bytes 2359328 | tf_op jit(solution)/shard_map/all_to_all | solution.py:16
  42.9 60.3 %while.24 = (s32[]{:T(128)}, f32[8,128]{1,0:T(8,128)S(1)}, f32[8,128]{1,0:T(8,128)S(1)}, f32[8,3,1536]{2,1,0:T(4,128)S(1)}, f32[3,128]{1,0:T(4,128)S(1)}, /*inde...) while((s32[]{:T(128)}, f32[8,128]{1,0:T(8,128)S(1)}, f32[8,128]{1,0:T(8,128)S(1)}, ...), condition=%wide.wide.region_3.4_spmd, body=%wide.wide.region_2.0_spmd.sunk | while | flops 11993090 | bytes 2401385 | solution.py:82
  42.9 1.4 convolution_multiply_fusion.7
  44.3 3.0 %fusion.81 = f32[1,128]{1,0:T(1,128)S(1)} fusion(f32[1536,1]{0,1:T(1,128)S(1)} %get-tuple-element.313, f32[1536,128]{1,0:T(8,128)S(1)} %convolution_multiply_fusion.7), kind=kOutput, calls=%fused_computation.3.clone.clone.1 | convolution fusion | flops 2359296 | bytes 793088 | tf_op jit(solution)/shard_map/while/body/eval_jaxpr/dot_general | solution.py:78
  47.4 3.0 %fusion.82 = f32[1,128]{1,0:T(1,128)S(1)} fusion(f32[1536,1]{0,1:T(1,128)S(1)} %get-tuple-element.313, f32[1536,128]{1,0:T(8,128)S(1)} %convolution_multiply_fusion.7), kind=kOutput, calls=%fused_computation.1.clone.clone.1 | convolution fusion | flops 2359296 | bytes 793088 | tf_op jit(solution)/shard_map/while/body/eval_jaxpr/dot_general | solution.py:79
  50.4 1.4 convolution_multiply_fusion.7
  51.9 3.0 %fusion.81 = f32[1,128]{1,0:T(1,128)S(1)} fusion(f32[1536,1]{0,1:T(1,128)S(1)} %get-tuple-element.313, f32[1536,128]{1,0:T(8,128)S(1)} %convolution_multiply_fusion.7), kind=kOutput, calls=%fused_computation.3.clone.clone.1 | convolution fusion | flops 2359296 | bytes 793088 | tf_op jit(solution)/shard_map/while/body/eval_jaxpr/dot_general | solution.py:78
  54.9 3.0 %fusion.82 = f32[1,128]{1,0:T(1,128)S(1)} fusion(f32[1536,1]{0,1:T(1,128)S(1)} %get-tuple-element.313, f32[1536,128]{1,0:T(8,128)S(1)} %convolution_multiply_fusion.7), kind=kOutput, calls=%fused_computation.1.clone.clone.1 | convolution fusion | flops 2359296 | bytes 793088 | tf_op jit(solution)/shard_map/while/body/eval_jaxpr/dot_general | solution.py:79
  58.0 1.4 convolution_multiply_fusion.7
  59.4 3.0 %fusion.81 = f32[1,128]{1,0:T(1,128)S(1)} fusion(f32[1536,1]{0,1:T(1,128)S(1)} %get-tuple-element.313, f32[1536,128]{1,0:T(8,128)S(1)} %convolution_multiply_fusion.7), kind=kOutput, calls=%fused_computation.3.clone.clone.1 | convolution fusion | flops 2359296 | bytes 793088 | tf_op jit(solution)/shard_map/while/body/eval_jaxpr/dot_general | solution.py:78
  62.4 3.0 %fusion.82 = f32[1,128]{1,0:T(1,128)S(1)} fusion(f32[1536,1]{0,1:T(1,128)S(1)} %get-tuple-element.313, f32[1536,128]{1,0:T(8,128)S(1)} %convolution_multiply_fusion.7), kind=kOutput, calls=%fused_computation.1.clone.clone.1 | convolution fusion | flops 2359296 | bytes 793088 | tf_op jit(solution)/shard_map/while/body/eval_jaxpr/dot_general | solution.py:79
  65.5 1.4 convolution_multiply_fusion.7
  66.9 3.0 %fusion.81 = f32[1,128]{1,0:T(1,128)S(1)} fusion(f32[1536,1]{0,1:T(1,128)S(1)} %get-tuple-element.313, f32[1536,128]{1,0:T(8,128)S(1)} %convolution_multiply_fusion.7), kind=kOutput, calls=%fused_computation.3.clone.clone.1 | convolution fusion | flops 2359296 | bytes 793088 | tf_op jit(solution)/shard_map/while/body/eval_jaxpr/dot_general | solution.py:78
  70.0 3.0 %fusion.82 = f32[1,128]{1,0:T(1,128)S(1)} fusion(f32[1536,1]{0,1:T(1,128)S(1)} %get-tuple-element.313, f32[1536,128]{1,0:T(8,128)S(1)} %convolution_multiply_fusion.7), kind=kOutput, calls=%fused_computation.1.clone.clone.1 | convolution fusion | flops 2359296 | bytes 793088 | tf_op jit(solution)/shard_map/while/body/eval_jaxpr/dot_general | solution.py:79
  73.0 1.4 convolution_multiply_fusion.7
  74.5 3.0 %fusion.81 = f32[1,128]{1,0:T(1,128)S(1)} fusion(f32[1536,1]{0,1:T(1,128)S(1)} %get-tuple-element.313, f32[1536,128]{1,0:T(8,128)S(1)} %convolution_multiply_fusion.7), kind=kOutput, calls=%fused_computation.3.clone.clone.1 | convolution fusion | flops 2359296 | bytes 793088 | tf_op jit(solution)/shard_map/while/body/eval_jaxpr/dot_general | solution.py:78
  77.5 3.0 %fusion.82 = f32[1,128]{1,0:T(1,128)S(1)} fusion(f32[1536,1]{0,1:T(1,128)S(1)} %get-tuple-element.313, f32[1536,128]{1,0:T(8,128)S(1)} %convolution_multiply_fusion.7), kind=kOutput, calls=%fused_computation.1.clone.clone.1 | convolution fusion | flops 2359296 | bytes 793088 | tf_op jit(solution)/shard_map/while/body/eval_jaxpr/dot_general | solution.py:79
  80.6 1.4 convolution_multiply_fusion.7
  82.0 3.0 %fusion.81 = f32[1,128]{1,0:T(1,128)S(1)} fusion(f32[1536,1]{0,1:T(1,128)S(1)} %get-tuple-element.313, f32[1536,128]{1,0:T(8,128)S(1)} %convolution_multiply_fusion.7), kind=kOutput, calls=%fused_computation.3.clone.clone.1 | convolution fusion | flops 2359296 | bytes 793088 | tf_op jit(solution)/shard_map/while/body/eval_jaxpr/dot_general | solution.py:78
  85.0 3.0 %fusion.82 = f32[1,128]{1,0:T(1,128)S(1)} fusion(f32[1536,1]{0,1:T(1,128)S(1)} %get-tuple-element.313, f32[1536,128]{1,0:T(8,128)S(1)} %convolution_multiply_fusion.7), kind=kOutput, calls=%fused_computation.1.clone.clone.1 | convolution fusion | flops 2359296 | bytes 793088 | tf_op jit(solution)/shard_map/while/body/eval_jaxpr/dot_general | solution.py:79
  88.1 1.4 convolution_multiply_fusion.7
  89.5 3.0 %fusion.81 = f32[1,128]{1,0:T(1,128)S(1)} fusion(f32[1536,1]{0,1:T(1,128)S(1)} %get-tuple-element.313, f32[1536,128]{1,0:T(8,128)S(1)} %convolution_multiply_fusion.7), kind=kOutput, calls=%fused_computation.3.clone.clone.1 | convolution fusion | flops 2359296 | bytes 793088 | tf_op jit(solution)/shard_map/while/body/eval_jaxpr/dot_general | solution.py:78
  92.6 3.0 %fusion.82 = f32[1,128]{1,0:T(1,128)S(1)} fusion(f32[1536,1]{0,1:T(1,128)S(1)} %get-tuple-element.313, f32[1536,128]{1,0:T(8,128)S(1)} %convolution_multiply_fusion.7), kind=kOutput, calls=%fused_computation.1.clone.clone.1 | convolution fusion | flops 2359296 | bytes 793088 | tf_op jit(solution)/shard_map/while/body/eval_jaxpr/dot_general | solution.py:79
  95.6 1.4 convolution_multiply_fusion.7
  97.1 3.0 %fusion.81 = f32[1,128]{1,0:T(1,128)S(1)} fusion(f32[1536,1]{0,1:T(1,128)S(1)} %get-tuple-element.313, f32[1536,128]{1,0:T(8,128)S(1)} %convolution_multiply_fusion.7), kind=kOutput, calls=%fused_computation.3.clone.clone.1 | convolution fusion | flops 2359296 | bytes 793088 | tf_op jit(solution)/shard_map/while/body/eval_jaxpr/dot_general | solution.py:78
  100.1 3.0 %fusion.82 = f32[1,128]{1,0:T(1,128)S(1)} fusion(f32[1536,1]{0,1:T(1,128)S(1)} %get-tuple-element.313, f32[1536,128]{1,0:T(8,128)S(1)} %convolution_multiply_fusion.7), kind=kOutput, calls=%fused_computation.1.clone.clone.1 | convolution fusion | flops 2359296 | bytes 793088 | tf_op jit(solution)/shard_map/while/body/eval_jaxpr/dot_general | solution.py:79
  103.2 0.7 broadcast_in_dim.34
  103.8 5.1 %all-to-all-start.1 = ((f32[8,1,2048]{2,1,0:T(1,128)}), f32[8,1,2048]{2,1,0:T(1,128)S(1)}, u32[]{:S(2)}, u32[]{:S(2)}) async-start(f32[8,1,2048]{2,1,0:T(1,128)} %broadcast_in_dim.34), calls=%async_computation.1 | async-start | bytes 131072 | tf_op jit(solution)/shard_map/all_to_all | solution.py:16
  109.0 5.2 %all-to-all-done.1 = f32[8,1,2048]{2,1,0:T(1,128)S(1)} async-done(((f32[8,1,2048]{2,1,0:T(1,128)}), f32[8,1,2048]{2,1,0:T(1,128)S(1)}, u32[]{:S(2)}, u32[]{:S(2)}) %all-to-all-start.1) | async-done | bytes 65568 | tf_op jit(solution)/shard_map/all_to_all | solution.py:16
  114.3 75.3 %while.23 = (s32[]{:T(128)}, f32[8,3,1536]{2,0,1:T(8,128)S(1)}, f32[1536]{0:T(1024)}, f32[128]{0:T(128)S(1)}, f32[8,128]{1,0:T(8,128)S(1)}, /*index=5*/f32[3,128...) while((s32[]{:T(128)}, f32[8,3,1536]{2,0,1:T(8,128)S(1)}, ...), condition=%wide.region_7.8_spmd, body=%wide.region_6.7_spmd.sunk | while | flops 21440768 | bytes 2527857 | solution.py:97
  114.3 1.4 convolution_multiply_fusion.6
  115.7 3.5 %fusion.73 = f32[3,1536]{1,0:T(4,128)S(1)} fusion(f32[1536,128]{1,0:T(8,128)S(1)} %convolution_multiply_fusion.6, f32[3,128]{1,0:T(4,128)S(1)} %get-tuple-element.341, f32[128]{0:T(128)S(1)} %get-tuple-element.280), kind=kOutput, calls=%fused_computation.15.clone.1 | convolution fusion | flops 7078272 | bytes 806912 | tf_op jit(solution)/shard_map/while/body/eval_jaxpr/dot_general | solution.py:92
  119.2 4.2 %fusion.74 = f32[1,3,1536]{2,1,0:T(4,128)S(1)} fusion(f32[3,1536]{1,0:T(4,128)S(1)} %fusion.73, f32[1536,128]{1,0:T(8,128)S(1)} %convolution_multiply_fusion.6, f32[1536]{0:T(1024)} %get-tuple-element.338, f32[3,128]{1,0:T(4,128)S(1)} %get-tuple-element.341, f32[128]{0:T(128)S(1)} %get-tuple-element.281), kind=kOutput, calls=%fused_computation.13.clone.1 | convolution fusion | flops 7087488 | bytes 831488 | tf_op jit(solution)/shard_map/while/body/eval_jaxpr/dot_general | solution.py:92
  123.5 0.2 dynamic_update_slice.16
  123.7 1.4 convolution_multiply_fusion.6
  125.1 3.5 %fusion.73 = f32[3,1536]{1,0:T(4,128)S(1)} fusion(f32[1536,128]{1,0:T(8,128)S(1)} %convolution_multiply_fusion.6, f32[3,128]{1,0:T(4,128)S(1)} %get-tuple-element.341, f32[128]{0:T(128)S(1)} %get-tuple-element.280), kind=kOutput, calls=%fused_computation.15.clone.1 | convolution fusion | flops 7078272 | bytes 806912 | tf_op jit(solution)/shard_map/while/body/eval_jaxpr/dot_general | solution.py:92
  128.6 4.2 %fusion.74 = f32[1,3,1536]{2,1,0:T(4,128)S(1)} fusion(f32[3,1536]{1,0:T(4,128)S(1)} %fusion.73, f32[1536,128]{1,0:T(8,128)S(1)} %convolution_multiply_fusion.6, f32[1536]{0:T(1024)} %get-tuple-element.338, f32[3,128]{1,0:T(4,128)S(1)} %get-tuple-element.341, f32[128]{0:T(128)S(1)} %get-tuple-element.281), kind=kOutput, calls=%fused_computation.13.clone.1 | convolution fusion | flops 7087488 | bytes 831488 | tf_op jit(solution)/shard_map/while/body/eval_jaxpr/dot_general | solution.py:92
  133.1 1.4 convolution_multiply_fusion.6
  134.5 3.5 %fusion.73 = f32[3,1536]{1,0:T(4,128)S(1)} fusion(f32[1536,128]{1,0:T(8,128)S(1)} %convolution_multiply_fusion.6, f32[3,128]{1,0:T(4,128)S(1)} %get-tuple-element.341, f32[128]{0:T(128)S(1)} %get-tuple-element.280), kind=kOutput, calls=%fused_computation.15.clone.1 | convolution fusion | flops 7078272 | bytes 806912 | tf_op jit(solution)/shard_map/while/body/eval_jaxpr/dot_general | solution.py:92
  138.0 4.2 %fusion.74 = f32[1,3,1536]{2,1,0:T(4,128)S(1)} fusion(f32[3,1536]{1,0:T(4,128)S(1)} %fusion.73, f32[1536,128]{1,0:T(8,128)S(1)} %convolution_multiply_fusion.6, f32[1536]{0:T(1024)} %get-tuple-element.338, f32[3,128]{1,0:T(4,128)S(1)} %get-tuple-element.341, f32[128]{0:T(128)S(1)} %get-tuple-element.281), kind=kOutput, calls=%fused_computation.13.clone.1 | convolution fusion | flops 7087488 | bytes 831488 | tf_op jit(solution)/shard_map/while/body/eval_jaxpr/dot_general | solution.py:92
  142.5 1.4 convolution_multiply_fusion.6
  144.0 3.5 %fusion.73 = f32[3,1536]{1,0:T(4,128)S(1)} fusion(f32[1536,128]{1,0:T(8,128)S(1)} %convolution_multiply_fusion.6, f32[3,128]{1,0:T(4,128)S(1)} %get-tuple-element.341, f32[128]{0:T(128)S(1)} %get-tuple-element.280), kind=kOutput, calls=%fused_computation.15.clone.1 | convolution fusion | flops 7078272 | bytes 806912 | tf_op jit(solution)/shard_map/while/body/eval_jaxpr/dot_general | solution.py:92
  147.5 4.2 %fusion.74 = f32[1,3,1536]{2,1,0:T(4,128)S(1)} fusion(f32[3,1536]{1,0:T(4,128)S(1)} %fusion.73, f32[1536,128]{1,0:T(8,128)S(1)} %convolution_multiply_fusion.6, f32[1536]{0:T(1024)} %get-tuple-element.338, f32[3,128]{1,0:T(4,128)S(1)} %get-tuple-element.341, f32[128]{0:T(128)S(1)} %get-tuple-element.281), kind=kOutput, calls=%fused_computation.13.clone.1 | convolution fusion | flops 7087488 | bytes 831488 | tf_op jit(solution)/shard_map/while/body/eval_jaxpr/dot_general | solution.py:92
  151.7 0.2 dynamic_update_slice.16
  151.9 1.4 convolution_multiply_fusion.6
  153.4 3.5 %fusion.73 = f32[3,1536]{1,0:T(4,128)S(1)} fusion(f32[1536,128]{1,0:T(8,128)S(1)} %convolution_multiply_fusion.6, f32[3,128]{1,0:T(4,128)S(1)} %get-tuple-element.341, f32[128]{0:T(128)S(1)} %get-tuple-element.280), kind=kOutput, calls=%fused_computation.15.clone.1 | convolution fusion | flops 7078272 | bytes 806912 | tf_op jit(solution)/shard_map/while/body/eval_jaxpr/dot_general | solution.py:92
  156.9 4.2 %fusion.74 = f32[1,3,1536]{2,1,0:T(4,128)S(1)} fusion(f32[3,1536]{1,0:T(4,128)S(1)} %fusion.73, f32[1536,128]{1,0:T(8,128)S(1)} %convolution_multiply_fusion.6, f32[1536]{0:T(1024)} %get-tuple-element.338, f32[3,128]{1,0:T(4,128)S(1)} %get-tuple-element.341, f32[128]{0:T(128)S(1)} %get-tuple-element.281), kind=kOutput, calls=%fused_computation.13.clone.1 | convolution fusion | flops 7087488 | bytes 831488 | tf_op jit(solution)/shard_map/while/body/eval_jaxpr/dot_general | solution.py:92
  161.4 1.4 convolution_multiply_fusion.6
  162.8 3.5 %fusion.73 = f32[3,1536]{1,0:T(4,128)S(1)} fusion(f32[1536,128]{1,0:T(8,128)S(1)} %convolution_multiply_fusion.6, f32[3,128]{1,0:T(4,128)S(1)} %get-tuple-element.341, f32[128]{0:T(128)S(1)} %get-tuple-element.280), kind=kOutput, calls=%fused_computation.15.clone.1 | convolution fusion | flops 7078272 | bytes 806912 | tf_op jit(solution)/shard_map/while/body/eval_jaxpr/dot_general | solution.py:92
  166.3 4.2 %fusion.74 = f32[1,3,1536]{2,1,0:T(4,128)S(1)} fusion(f32[3,1536]{1,0:T(4,128)S(1)} %fusion.73, f32[1536,128]{1,0:T(8,128)S(1)} %convolution_multiply_fusion.6, f32[1536]{0:T(1024)} %get-tuple-element.338, f32[3,128]{1,0:T(4,128)S(1)} %get-tuple-element.341, f32[128]{0:T(128)S(1)} %get-tuple-element.281), kind=kOutput, calls=%fused_computation.13.clone.1 | convolution fusion | flops 7087488 | bytes 831488 | tf_op jit(solution)/shard_map/while/body/eval_jaxpr/dot_general | solution.py:92
  170.8 1.4 convolution_multiply_fusion.6
  172.2 3.5 %fusion.73 = f32[3,1536]{1,0:T(4,128)S(1)} fusion(f32[1536,128]{1,0:T(8,128)S(1)} %convolution_multiply_fusion.6, f32[3,128]{1,0:T(4,128)S(1)} %get-tuple-element.341, f32[128]{0:T(128)S(1)} %get-tuple-element.280), kind=kOutput, calls=%fused_computation.15.clone.1 | convolution fusion | flops 7078272 | bytes 806912 | tf_op jit(solution)/shard_map/while/body/eval_jaxpr/dot_general | solution.py:92
  175.7 4.2 %fusion.74 = f32[1,3,1536]{2,1,0:T(4,128)S(1)} fusion(f32[3,1536]{1,0:T(4,128)S(1)} %fusion.73, f32[1536,128]{1,0:T(8,128)S(1)} %convolution_multiply_fusion.6, f32[1536]{0:T(1024)} %get-tuple-element.338, f32[3,128]{1,0:T(4,128)S(1)} %get-tuple-element.341, f32[128]{0:T(128)S(1)} %get-tuple-element.281), kind=kOutput, calls=%fused_computation.13.clone.1 | convolution fusion | flops 7087488 | bytes 831488 | tf_op jit(solution)/shard_map/while/body/eval_jaxpr/dot_general | solution.py:92
  180.2 1.4 convolution_multiply_fusion.6
  181.6 3.5 %fusion.73 = f32[3,1536]{1,0:T(4,128)S(1)} fusion(f32[1536,128]{1,0:T(8,128)S(1)} %convolution_multiply_fusion.6, f32[3,128]{1,0:T(4,128)S(1)} %get-tuple-element.341, f32[128]{0:T(128)S(1)} %get-tuple-element.280), kind=kOutput, calls=%fused_computation.15.clone.1 | convolution fusion | flops 7078272 | bytes 806912 | tf_op jit(solution)/shard_map/while/body/eval_jaxpr/dot_general | solution.py:92
  185.1 4.2 %fusion.74 = f32[1,3,1536]{2,1,0:T(4,128)S(1)} fusion(f32[3,1536]{1,0:T(4,128)S(1)} %fusion.73, f32[1536,128]{1,0:T(8,128)S(1)} %convolution_multiply_fusion.6, f32[1536]{0:T(1024)} %get-tuple-element.338, f32[3,128]{1,0:T(4,128)S(1)} %get-tuple-element.341, f32[128]{0:T(128)S(1)} %get-tuple-element.281), kind=kOutput, calls=%fused_computation.13.clone.1 | convolution fusion | flops 7087488 | bytes 831488 | tf_op jit(solution)/shard_map/while/body/eval_jaxpr/dot_general | solution.py:92
  189.4 0.2 dynamic_update_slice.16
  189.8 16.6 %all_to_all.34 = f32[16,8,3,96]{3,1,2,0:T(8,128)S(1)} all-to-all(f32[16,8,3,96]{3,1,2,0:T(8,128)S(1)} %copy.37), channel_id=1, replica_groups=mesh['bead'=16,'atom'=8] {'bead'}, dimensions={0} | all-to-all | bytes 294912 | tf_op jit(solution)/shard_map/all_to_all | solution.py:40
  206.4 0.4 fusion.29
  207.0 11.7 %all_to_all.35 = f32[128,3,96]{2,1,0:T(4,128)S(1)} all-to-all(f32[128,3,96]{2,1,0:T(4,128)S(1)} %copy.38), channel_id=1, replica_groups=mesh['bead'=16,'atom'=8] {'bead'}, dimensions={0} | all-to-all | bytes 294912 | tf_op jit(solution)/shard_map/all_to_all | solution.py:129
  218.8 0.8 all_to_all.29
  (79 shorter events, 3.5 us)
Async XLA Ops:
  0.0 0.9 copy-start
  3.0 8.6 %copy-start.3 = (s32[1536]{0:T(1024)S(1)}, s32[1536]{0:T(1024)}, u32[]{:S(2)}) copy-start(s32[1536]{0:T(1024)} %param.10) | copy-start | bytes 18436
  3.0 8.6 %copy-start.4 = (f32[4]{0:T(128)S(1)}, f32[4]{0:T(128)}, u32[]{:S(2)}) copy-start(f32[4]{0:T(128)} %param.11) | copy-start | bytes 52
  3.0 8.7 %copy-start.2 = (s32[3,128]{1,0:T(4,128)S(1)}, s32[3,128]{1,0:T(4,128)}, u32[]{:S(2)}) copy-start(s32[3,128]{1,0:T(4,128)} %param.9) | copy-start | bytes 4612
  3.0 39.7 %all-to-all-start = ((f32[16,8,3,1536]{3,1,2,0:T(8,128)}), f32[16,8,3,1536]{3,1,2,0:T(8,128)S(1)}, u32[]{:S(2)}, u32[]{:S(2)}) async-start(f32[16,8,3,1536]{3,1,2,0:T(8,128)} %broadcast_in_dim.17), calls=%async_computation | async-start | bytes 4718592 | tf_op jit(solution)/shard_map/all_to_all | solution.py:16
  11.7 31.2 %copy-start.1 = (f32[1536]{0:T(1024)}, f32[1536]{0:T(1024)S(1)}, u32[]{:S(2)}) copy-start(f32[1536]{0:T(1024)S(1)} %select_reduce_fusion) | copy-start | bytes 18436
  103.8 10.3 %all-to-all-start.1 = ((f32[8,1,2048]{2,1,0:T(1,128)}), f32[8,1,2048]{2,1,0:T(1,128)S(1)}, u32[]{:S(2)}, u32[]{:S(2)}) async-start(f32[8,1,2048]{2,1,0:T(1,128)} %broadcast_in_dim.34), calls=%async_computation.1 | async-start | bytes 131072 | tf_op jit(solution)/shard_map/all_to_all | solution.py:16
where the time goes:
time: 220 us
  matrix products  133 us (60%)
  waiting for transfers between devices  36.1 us (16%)
  blocking collectives  28.4 us (13%)
  starting transfers between devices  13.7 us (6%)
  local copies, waits for them, and re-layouts  6.15 us (3%)
    all_to_all x2, waiting for transfers between devices, copy_for_each(): lax.all_to_all(jnp.broadcast_to(array[None], (peers, *array.shape)), axis...  36.1 us
    dot_general x8, matrix products, forces(): jnp.dot(right, jnp.cos(angle), precision=lax.Precision.HIGHEST)  33.8 us
    dot_general x8, matrix products, forces(): jnp.dot(left, jnp.sin(angle), precision=lax.Precision.HIGHEST)  28 us
    dot_general x8, matrix products, structure(): jnp.dot(jnp.sin(angle), charge, precision=lax.Precision.HIGHEST)  24.2 us
    dot_general x8, matrix products, structure(): jnp.dot(jnp.cos(angle), charge, precision=lax.Precision.HIGHEST)  23.9 us
    dot_general x16, matrix products, phases(): jnp.dot(fourier_mode_table.T, position, precision=lax.Precision.HIGHEST)  22.6 us
    all_to_all x1, blocking collectives, summed_on_arrival(): lax.all_to_all(in_blocks(array, dim, peers), axis, 0, 0, tiled=True)  16.6 us
    all_to_all x2, starting transfers between devices, copy_for_each(): lax.all_to_all(jnp.broadcast_to(array[None], (peers, *array.shape)), axis...  13.7 us
  transfers between devices with their start and end apart: 2, of which 2 were waited for; matrix products, arithmetic and copies ran while one was open for 0% of the time, Pallas kernels for 0%

commit v1 on v0

v1 whole, which is shorter than its diff:
```python
import functools
import math

import jax
import jax.numpy as jnp
import numpy as np
from jax import lax
from jax.experimental import pallas as pl
from jax.experimental.pallas import tpu as pltpu
from jax.sharding import PartitionSpec as P

CONTR = 8
TOP = 10
SIDE = 2 * TOP + 1
PAIRS = (TOP + 1) * SIDE
HALF = (PAIRS + 1) // 2
LANES = 128
ROWS = 16
SENT = 12
TWO_PI = 2.0 * math.pi


def polynomials():
    nodes = 0.5 * np.cos(np.pi * (np.arange(400) + 0.5) / 400)
    u = nodes * nodes
    odd = np.linalg.lstsq(
        nodes[:, None] * u[:, None] ** np.arange(7), np.sin(2 * np.pi * nodes), rcond=None
    )[0]
    even = np.linalg.lstsq(u[:, None] ** np.arange(8), np.cos(2 * np.pi * nodes), rcond=None)[0]
    return [float(c) for c in odd], [float(c) for c in even]


ODD, EVEN = polynomials()


def horner(u, coefficients):
    total = coefficients[-1]
    for c in coefficients[-2::-1]:
        total = total * u + c
    return total


def reduced(t):
    return t - jnp.round(t)


def sin_turns(t):
    t = reduced(t)
    return t * horner(t * t, ODD)


def both_turns(t):
    t = reduced(t)
    u = t * t
    return horner(u, EVEN), t * horner(u, ODD)


def cycle_modes(length, count):
    index = np.arange(length, dtype=np.float64)
    rows = [np.ones(length) / math.sqrt(length)]
    for mode in range(1, count // 2):
        rows.append(math.sqrt(2.0 / length) * np.cos(TWO_PI * mode * index / length))
        rows.append(math.sqrt(2.0 / length) * np.sin(TWO_PI * mode * index / length))
    if length == count:
        rows.append(np.cos(math.pi * index) / math.sqrt(length))
    else:
        rows.append(math.sqrt(2.0 / length) * np.cos(TWO_PI * (count // 2) * index / length))
    return np.stack(rows)


def contraction_table(beads, contr):
    small = cycle_modes(contr, contr)
    big = cycle_modes(beads, contr)
    return (math.sqrt(contr / beads) * small.T @ big).astype(np.float32)


def iota(shape, dim):
    return lax.broadcasted_iota(jnp.int32, shape, dim).astype(jnp.float32)


def pair_of(index):
    m2 = jnp.floor((index + 0.5) * (1.0 / SIDE))
    return m2, index - m2 * SIDE - TOP


def split(value):
    high = value.astype(jnp.bfloat16)
    low = (value - high.astype(jnp.float32)).astype(jnp.bfloat16)
    return high, low


def dot_nt(a, b):
    return lax.dot_general(a, b, (((1,), (1,)), ((), ())), preferred_element_type=jnp.float32)


def contract_kernel(table_ref, points_ref, waves_ref, out_ref, work_ref):
    beads = points_ref.shape[1]
    tiles = points_ref.shape[2] // LANES
    columns = [
        jnp.broadcast_to(table_ref[:, b : b + 1], (CONTR, LANES)) for b in range(beads)
    ]
    for x in range(3):
        for t in range(tiles):
            block = points_ref[x, :, t * LANES : (t + 1) * LANES]
            total = columns[0] * jnp.broadcast_to(block[0:1], (CONTR, LANES))
            for b in range(1, beads):
                total += columns[b] * jnp.broadcast_to(block[b : b + 1], (CONTR, LANES))
            row = (x * tiles + t) * CONTR
            work_ref[row : row + CONTR, :] = total
    waves = waves_ref[...].astype(jnp.float32)
    used = 3 * tiles
    copies = out_ref.shape[0] // CONTR
    for j in range(CONTR):
        rows = work_ref[pl.ds(j, used, stride=CONTR), :]
        for c in range(copies):
            out_ref[j * copies + c, 0:used, :] = rows
            out_ref[j * copies + c, used : used + 3, :] = waves


def structure_kernel(
    number_points,
    spots_ref,
    labels_ref,
    species_ref,
    partial_ref,
    weights_ref,
    high_ref,
    low_ref,
    plain_ref,
    slope_ref,
    charged_ref,
):
    core = lax.rem(lax.axis_index("bead"), 2).astype(jnp.float32)
    peers = spots_ref.shape[0]
    tiles = labels_ref.shape[0]
    used = 3 * tiles
    spots = spots_ref[0, 0:used, :]
    for p in range(1, peers):
        spots += spots_ref[p, 0:used, :]
    spots = reduced(spots)
    labels = labels_ref[...]
    charge = jnp.zeros(labels.shape, jnp.float32)
    for kind in range(species_ref.shape[0]):
        charge += jnp.where(labels == kind, species_ref[kind], 0.0)
    first = core * HALF
    grid_row = iota((2 * ROWS, LANES), 0)
    back = grid_row >= ROWS
    size = jnp.where(back, grid_row - ROWS, grid_row)
    wanted = jnp.where(back, jnp.where(size > 0, -size, 1000.0), size)
    pair_row = iota((LANES, LANES), 0)
    counts = jnp.zeros((2 * ROWS, LANES), jnp.float32)
    for p in range(peers):
        m1 = spots_ref[p, used : used + 1, :]
        m2 = spots_ref[p, used + 1 : used + 2, :]
        m3 = spots_ref[p, used + 2 : used + 3, :]
        sign = jnp.where(m2 < 0, -1.0, 1.0)
        place = (m2 * sign) * SIDE + (m3 * sign) + TOP - first
        place = jnp.where(place < HALF, place, -1.0)
        left = jnp.where(wanted == m1 * sign, 1.0, 0.0).astype(jnp.bfloat16)
        right = jnp.where(pair_row == place, 1.0, 0.0).astype(jnp.bfloat16)
        counts += dot_nt(left, right)
    m2, m3 = pair_of(iota((2 * ROWS, LANES), 1) + first)
    square = size * size + m2 * m2 + m3 * m3
    square = jnp.maximum(square, 1.0)
    weights_ref[...] = counts * (4.0 * jnp.exp(square * -0.01) / (square * number_points))
    row = iota((2 * ROWS, LANES), 0)
    sine = row >= ROWS
    m1 = jnp.where(sine, row - ROWS, row)
    phase = jnp.where(sine, 0.0, 0.25)
    chunk = 32
    for t in range(tiles):
        lanes = slice(t * LANES, (t + 1) * LANES)
        x1 = spots[t : t + 1, :]
        q = charge[t : t + 1, :]
        angle = m1 * x1 + phase
        plain = q * sin_turns(angle)
        plain_ref[:, lanes] = plain
        slope_ref[:, lanes] = (q * (-TWO_PI)) * m1 * sin_turns(angle + 0.25)
        high, low = split(plain)
        charged_ref[0 : 2 * ROWS, lanes] = high
        charged_ref[2 * ROWS :, lanes] = low
    for r in range(0, LANES, chunk):
        m2, m3 = pair_of(iota((chunk, LANES), 0) + (first + r))
        for t in range(tiles):
            lanes = slice(t * LANES, (t + 1) * LANES)
            x2 = spots[tiles + t : tiles + t + 1, :]
            x3 = spots[2 * tiles + t : 2 * tiles + t + 1, :]
            cosine, sine = both_turns(m2 * x2 + m3 * x3)
            high, low = split(cosine)
            high_ref[r : r + chunk, lanes] = high
            low_ref[r : r + chunk, lanes] = low
            high, low = split(sine)
            high_ref[LANES + r : LANES + r + chunk, lanes] = high
            low_ref[LANES + r : LANES + r + chunk, lanes] = low
    total = dot_nt(charged_ref[...], high_ref[...])
    total = (
        total[0 : 2 * ROWS]
        + total[2 * ROWS :]
        + dot_nt(charged_ref[0 : 2 * ROWS, :], low_ref[...])
    )
    for p in range(partial_ref.shape[0]):
        partial_ref[p, 0:SENT, :] = total[0:SENT]
        partial_ref[p, SENT:, :] = total[ROWS : ROWS + SENT]


def force_kernel(
    partial_ref, weights_ref, high_ref, low_ref, plain_ref, slope_ref, out_ref, coef_ref, term_ref
):
    core = lax.rem(lax.axis_index("bead"), 2).astype(jnp.float32)
    tiles = plain_ref.shape[1] // LANES
    cos_row = partial_ref[0, 0:SENT, :]
    sin_row = partial_ref[0, SENT:, :]
    for p in range(1, partial_ref.shape[0]):
        cos_row += partial_ref[p, 0:SENT, :]
        sin_row += partial_ref[p, SENT:, :]
    ahead = weights_ref[0:SENT, :]
    back = weights_ref[ROWS : ROWS + SENT, :]
    cc, cs = cos_row[:, :LANES], cos_row[:, LANES:]
    sc, ss = sin_row[:, :LANES], sin_row[:, LANES:]
    ahead_cos, ahead_sin = ahead * (cc - ss), ahead * (cs + sc)
    back_cos, back_sin = back * (cc + ss), back * (cs - sc)
    m2, m3 = pair_of(iota((SENT, LANES), 1) + core * HALF)
    coef_ref[...] = jnp.zeros_like(coef_ref)
    rows = (
        (ahead_cos + back_cos, ahead_sin + back_sin),
        (ahead_sin - back_sin, back_cos - ahead_cos),
    )
    for kind, (on_cos, on_sin) in enumerate(rows):
        at = kind * ROWS
        coef_ref[at : at + SENT, :LANES] = on_cos
        coef_ref[at : at + SENT, LANES:] = on_sin
        for axis, m in enumerate((m2, m3)):
            at = kind * ROWS + 2 * ROWS * (axis + 1)
            coef_ref[at : at + SENT, :LANES] = (-TWO_PI) * m * on_sin
            coef_ref[at : at + SENT, LANES:] = TWO_PI * m * on_cos
    high, low = split(coef_ref[...])
    both = jnp.concatenate([high, low], axis=0)
    size = high.shape[0]
    width = 2 * LANES
    for t in range(0, tiles, 2):
        lanes = slice(t * LANES, t * LANES + width)
        near = jnp.dot(both, high_ref[:, lanes], preferred_element_type=jnp.float32)
        far = jnp.dot(high, low_ref[:, lanes], preferred_element_type=jnp.float32)
        term = near[:size] + near[size:] + far
        plain = plain_ref[:, lanes]
        values = [term[0 : 2 * ROWS] * slope_ref[:, lanes]]
        for axis in range(2):
            at = 2 * ROWS * (axis + 1)
            values.append(term[at : at + 2 * ROWS] * plain)
        for x, value in enumerate(values):
            total = jnp.sum(value, axis=0, keepdims=True)
            for i in range(2):
                term_ref[x * tiles + t + i : x * tiles + t + i + 1, :] = total[
                    :, i * LANES : (i + 1) * LANES
                ]
    block = term_ref[...]
    for p in range(out_ref.shape[0]):
        out_ref[p, 0 : block.shape[0], :] = block


def expand_kernel(table_ref, force_ref, out_ref, work_ref):
    beads = out_ref.shape[1]
    tiles = out_ref.shape[2] // LANES
    used = 3 * tiles
    stride = work_ref.shape[0] // beads
    copies = force_ref.shape[0] // CONTR
    parts = []
    for j in range(CONTR):
        part = force_ref[j * copies, 0:used, :]
        for c in range(1, copies):
            part += force_ref[j * copies + c, 0:used, :]
        parts.append(part)
    for b in range(beads):
        total = parts[0] * table_ref[b, 0]
        for j in range(1, CONTR):
            total += parts[j] * table_ref[b, j]
        work_ref[b * stride : b * stride + used, :] = total
    for x in range(3):
        for t in range(tiles):
            out_ref[x, :, t * LANES : (t + 1) * LANES] = work_ref[
                pl.ds(x * tiles + t, beads, stride=stride), :
            ]


VMEM = pl.BlockSpec(memory_space=pltpu.VMEM)
SMEM = pl.BlockSpec(memory_space=pltpu.SMEM)
PARAMS = pltpu.CompilerParams(vmem_limit_bytes=24 * 1024 * 1024)


def shaped(*shape, dtype=jnp.float32):
    return jax.ShapeDtypeStruct(shape, dtype)


def local(points, waves, labels, species):
    beads, _, sites = points.shape
    bead_peers = lax.axis_size("bead")
    atom_peers = lax.axis_size("atom")
    tiles = sites // LANES
    used = 3 * tiles
    sent = -(-(used + 3) // 8) * 8
    held = -(-used // 8) * 8
    table = contraction_table(beads * bead_peers, CONTR)
    blocks = jnp.asarray(table.reshape(CONTR, bead_peers, beads).transpose(1, 0, 2))
    mine = lax.dynamic_index_in_dim(blocks, lax.axis_index("bead"), 0, keepdims=False)
    portion = pl.pallas_call(
        contract_kernel,
        out_shape=shaped(bead_peers, sent, LANES),
        in_specs=[VMEM] * 3,
        out_specs=VMEM,
        scratch_shapes=[pltpu.VMEM((used * CONTR, LANES), jnp.float32)],
        compiler_params=PARAMS,
        name="contract",
    )(mine, points.transpose(1, 0, 2), waves)
    spots = lax.all_to_all(portion, "bead", 0, 0, tiled=True)
    partial, weights, high, low, plain, slope = pl.pallas_call(
        functools.partial(structure_kernel, float(sites * atom_peers)),
        out_shape=[
            shaped(atom_peers, 2 * SENT, 2 * LANES),
            shaped(2 * ROWS, LANES),
            shaped(2 * LANES, sites, dtype=jnp.bfloat16),
            shaped(2 * LANES, sites, dtype=jnp.bfloat16),
            shaped(2 * ROWS, sites),
            shaped(2 * ROWS, sites),
        ],
        in_specs=[VMEM, VMEM, SMEM],
        out_specs=[VMEM] * 6,
        scratch_shapes=[pltpu.VMEM((4 * ROWS, sites), jnp.bfloat16)],
        compiler_params=PARAMS,
        name="structure",
    )(spots, labels.reshape(tiles, LANES), species)
    factors = lax.all_to_all(partial, "atom", 0, 0, tiled=True)
    force = pl.pallas_call(
        force_kernel,
        out_shape=shaped(bead_peers, held, LANES),
        in_specs=[VMEM] * 6,
        out_specs=VMEM,
        scratch_shapes=[
            pltpu.VMEM((6 * ROWS, 2 * LANES), jnp.float32),
            pltpu.VMEM((used, LANES), jnp.float32),
        ],
        compiler_params=PARAMS,
        name="force",
    )(factors, weights, high, low, plain, slope)
    forces = lax.all_to_all(force, "bead", 0, 0, tiled=True)
    out = pl.pallas_call(
        expand_kernel,
        out_shape=shaped(3, beads, sites),
        in_specs=[SMEM, VMEM],
        out_specs=VMEM,
        scratch_shapes=[pltpu.VMEM((beads * held, LANES), jnp.float32)],
        compiler_params=PARAMS,
        name="expand",
    )(mine.T, forces)
    return out.transpose(1, 0, 2)


def solution(mesh):
    in_specs = (P("bead", None, "atom"), P(None, "bead"), P("atom"), P())
    out_specs = P("bead", None, "atom")
    return jax.shard_map(local, mesh=mesh, in_specs=in_specs, out_specs=out_specs, check_vma=False)
```

time: 220 us -> 51.1 us (0.23)
  matrix products: 133 us -> 0 us
  waiting for transfers between devices: 36.1 us -> 9.42 us
  starting transfers between devices: 13.7 us -> 5.14 us
  Pallas kernels: 0 us -> 5.26 us
  local copies, waits for them, and re-layouts: 6.15 us -> 2.34 us
    dot_general x51 -> x0, matrix products: 133 us -> none  [the longest x8 33.8 us: forces(): jnp.dot(right, jnp.cos(angle), precision=lax.Precision.HIGHEST)]
    all_to_all x2 -> x1, waiting for transfers between devices: 36.1 us -> 9.42 us  [local(): forces = lax.all_to_all(force, 'bead', 0, 0, tiled=True)]
    all_to_all x2 -> x1, starting transfers between devices: 13.7 us -> 5.14 us  [local(): forces = lax.all_to_all(force, 'bead', 0, 0, tiled=True)]
    pallas_call x0 -> x4, Pallas kernels: none -> 5.26 us  [the longest x1 2.49 us: local(): pl.pallas_call(functools.partial(structure_kernel, float(sites * atom_pee...]
    broadcast_in_dim x2 -> x0, local copies, waits for them, and re-layouts: 2.36 us -> none  [copy_for_each(): jnp.broadcast_to(array[None], (peers, *array.shape))]
    dynamic_update_slice x32 -> x0, local copies, waits for them, and re-layouts: 2.27 us -> none  [the longest x16 1.78 us: force_parts(): return lax.map(forces, (contracted, cos_fac, sin_fac))]
  transfers between devices with their start and end apart: 2 -> 1, of which waited for: 2 -> 1; matrix products, arithmetic and copies ran while one was open for 0% -> 0% of each run, Pallas kernels for 0% -> 0%
where the time goes in v1:
time: 51.1 us; the launch traced here: 50.8 us
  blocking collectives  28.6 us (56%)
  waiting for transfers between devices  9.42 us (18%)
  Pallas kernels  5.26 us (10%)
  starting transfers between devices  5.14 us (10%)
  local copies, waits for them, and re-layouts  2.34 us (5%)
    all_to_all x1, blocking collectives, local(): spots = lax.all_to_all(portion, 'bead', 0, 0, tiled=True)  17.7 us
    all_to_all x1, blocking collectives, local(): factors = lax.all_to_all(partial, 'atom', 0, 0, tiled=True)  10.9 us
    all_to_all x1, waiting for transfers between devices, local(): forces = lax.all_to_all(force, 'bead', 0, 0, tiled=True)  9.42 us
    all_to_all x1, starting transfers between devices, local(): forces = lax.all_to_all(force, 'bead', 0, 0, tiled=True)  5.14 us
    pallas_call x1, Pallas kernels, local(): pl.pallas_call(functools.partial(structure_kernel, float(sites * atom_pee...  2.49 us
    unnamed x8, local copies, waits for them, and re-layouts  1.57 us
    pallas_call x1, Pallas kernels, local(): pl.pallas_call(expand_kernel, out_shape=shaped(3, beads, sites), in_specs...  1.38 us
    pallas_call x1, Pallas kernels, local(): pl.pallas_call(force_kernel, out_shape=shaped(bead_peers, held, LANES), i...  1.21 us
  transfers between devices with their start and end apart: 1, of which 1 were waited for; matrix products, arithmetic and copies ran while one was open for 0% of the time, Pallas kernels for 0%

profile of v1, /device:TPU:1, one launch (start us, length us, event | category | flops | bytes accessed | tf_op | source)
XLA Modules:
  0.0 50.8 jit_solution(13631411591069739611)
XLA Ops:
  0.0 0.0 copy-start.2
  0.0 0.7 %dynamic-slice_bitcast_fusion.table_ref = f32[8,8]{1,0:T(8,128)S(1)} fusion(f32[16,8,8]{2,1,0:T(8,128)} %constant.14.clone, s32[]{:T(128)S(6)} %select_n.4), kind=kLoop, calls=%fused_computation | loop fusion | bytes 516 | tf_op jit(solution)/shard_map/jit(dynamic_index_in_dim)/squeeze | solution.py:304
  0.7 0.0 copy-done.2
  0.7 0.0 copy-start
  0.7 0.9 %copy-done = f32[8,3,1536]{2,0,1:T(8,128)S(1)} copy-done((f32[8,3,1536]{2,0,1:T(8,128)S(1)}, f32[8,3,1536]{2,0,1:T(8,128)}, u32[]{:S(2)}) %copy-start) | copy-done | bytes 147480
  1.6 0.2 contract.1
  1.8 0.0 copy-start.1
  1.8 17.7 %all_to_all.15.spots_ref = f32[16,40,128]{2,1,0:T(8,128)S(1)} all-to-all(f32[16,40,128]{2,1,0:T(8,128)S(1)} %contract.1), channel_id=1, replica_groups=mesh['bead'=16,'atom'=8] {'bead'}, dimensions={0} | all-to-all | bytes 655360 | tf_op jit(solution)/shard_map/all_to_all | solution.py:314
  19.5 0.0 copy-start.3
  19.5 0.0 copy-done.1
  19.5 0.7 %copy-done.3 = f32[4]{0:T(128)S(1)} copy-done((f32[4]{0:T(128)S(1)}, f32[4]{0:T(128)}, u32[]{:S(2)}) %copy-start.3) | copy-done | bytes 40
  20.2 2.5 %structure.1 = (f32[8,24,256]{2,1,0:T(8,128)S(1)}, f32[32,128]{1,0:T(8,128)S(1)}, bf16[256,1536]{1,0:T(8,128)(2,1)S(1)}, bf16[256,1536]{1,0:T(8,128)(2,1)S(1)}, ...) custom-call(f32[16,40,128]{2,1,0:T(8,128)S(1)} %all_to_all.15.spots_ref, s32[12,128]{1,0:T(8,128)S(1)} %bitcast.8, ...), custom_call_target="tpu_custom_call" | custom-call | tf_op jit(solution)/shard_map/structure/pallas_call | solution.py:315
  22.7 10.9 %all_to_all.16.partial_ref = f32[8,24,256]{2,1,0:T(8,128)S(1)} all-to-all(f32[8,24,256]{2,1,0:T(8,128)S(1)} %get-tuple-element.11), channel_id=1, replica_groups=mesh['bead'=16,'atom'=8] {'atom'}, dimensions={0} | all-to-all | bytes 393216 | tf_op jit(solution)/shard_map/all_to_all | solution.py:331
  33.5 1.2 %force.1 = f32[16,40,128]{2,1,0:T(8,128)} custom-call(f32[8,24,256]{2,1,0:T(8,128)S(1)} %all_to_all.16.partial_ref, f32[32,128]{1,0:T(8,128)S(1)} %get-tuple-element.12.weights_ref, bf16[256,1536]{1,0:T(8,128)(2,1)S(1)} %get-tuple-element.13.high_ref, bf16[256,1536]{1,0:T(8,128)(2,1)S(1)} %get-tuple-element.14.low_ref, ...), custom_call_target="tpu_custom_call" | custom-call | tf_op jit(solution)/shard_map/force/pallas_call | solution.py:332
  34.8 5.1 %all-to-all-start.2 = ((f32[16,40,128]{2,1,0:T(8,128)}), f32[16,40,128]{2,1,0:T(8,128)S(1)}, u32[]{:S(2)}, u32[]{:S(2)}) async-start(f32[16,40,128]{2,1,0:T(8,128)} %force.1), calls=%async_computation.2 | async-start | bytes 655360 | tf_op jit(solution)/shard_map/all_to_all | solution.py:344
  39.9 0.1 copy.6
  40.0 9.4 %all-to-all-done.2.force_ref = f32[16,40,128]{2,1,0:T(8,128)S(1)} async-done(((f32[16,40,128]{2,1,0:T(8,128)}), f32[16,40,128]{2,1,0:T(8,128)S(1)}, u32[]{:S(2)}, u32[]{:S(2)}) %all-to-all-start.2) | async-done | bytes 327712 | tf_op jit(solution)/shard_map/all_to_all | solution.py:344
  49.4 1.4 %expand.1 = f32[3,8,1536]{2,1,0:T(8,128)} custom-call(f32[8,8]{1,0:T(8,128)S(1)} %bitcast.7, f32[16,40,128]{2,1,0:T(8,128)S(1)} %all-to-all-done.2.force_ref), custom_call_target="tpu_custom_call" | custom-call | tf_op jit(solution)/shard_map/expand/pallas_call | solution.py:345
Async XLA Ops:
  0.0 0.7 %copy-start.2 = (s32[3,128]{1,0:T(4,128)S(1)}, s32[3,128]{1,0:T(4,128)}, u32[]{:S(2)}) copy-start(s32[3,128]{1,0:T(4,128)} %waves_ref.1) | copy-start | bytes 4612
  0.7 0.9 %copy-start = (f32[8,3,1536]{2,0,1:T(8,128)S(1)}, f32[8,3,1536]{2,0,1:T(8,128)}, u32[]{:S(2)}) copy-start(f32[8,3,1536]{2,0,1:T(8,128)} %param.5) | copy-start | bytes 442372
  1.8 17.7 %copy-start.1 = (s32[1536]{0:T(1024)S(1)}, s32[1536]{0:T(1024)}, u32[]{:S(2)}) copy-start(s32[1536]{0:T(1024)} %param.7) | copy-start | bytes 18436
  19.5 0.7 %copy-start.3 = (f32[4]{0:T(128)S(1)}, f32[4]{0:T(128)}, u32[]{:S(2)}) copy-start(f32[4]{0:T(128)} %species_ref.1) | copy-start | bytes 52
  34.8 14.6 %all-to-all-start.2 = ((f32[16,40,128]{2,1,0:T(8,128)}), f32[16,40,128]{2,1,0:T(8,128)S(1)}, u32[]{:S(2)}, u32[]{:S(2)}) async-start(f32[16,40,128]{2,1,0:T(8,128)} %force.1), calls=%async_computation.2 | async-start | bytes 655360 | tf_op jit(solution)/shard_map/all_to_all | solution.py:344

commit v2 on v1

--- a/solution.py
+++ b/solution.py
@@ -10,10 +10,6 @@
 from jax.sharding import PartitionSpec as P
 
 CONTR = 8
-TOP = 10
-SIDE = 2 * TOP + 1
-PAIRS = (TOP + 1) * SIDE
-HALF = (PAIRS + 1) // 2
 LANES = 128
 ROWS = 16
 SENT = 12
@@ -49,38 +45,47 @@
     return t * horner(t * t, ODD)
 
 
+def cos_turns(t):
+    t = reduced(t)
+    return horner(t * t, EVEN)
+
+
 def both_turns(t):
     t = reduced(t)
     u = t * t
     return horner(u, EVEN), t * horner(u, ODD)
 
 
-def cycle_modes(length, count):
-    index = np.arange(length, dtype=np.float64)
-    rows = [np.ones(length) / math.sqrt(length)]
-    for mode in range(1, count // 2):
-        rows.append(math.sqrt(2.0 / length) * np.cos(TWO_PI * mode * index / length))
-        rows.append(math.sqrt(2.0 / length) * np.sin(TWO_PI * mode * index / length))
-    if length == count:
-        rows.append(np.cos(math.pi * index) / math.sqrt(length))
-    else:
-        rows.append(math.sqrt(2.0 / length) * np.cos(TWO_PI * (count // 2) * index / length))
-    return np.stack(rows)
-
-
-def contraction_table(beads, contr):
-    small = cycle_modes(contr, contr)
-    big = cycle_modes(beads, contr)
-    return (math.sqrt(contr / beads) * small.T @ big).astype(np.float32)
-
-
 def iota(shape, dim):
     return lax.broadcasted_iota(jnp.int32, shape, dim).astype(jnp.float32)
 
 
-def pair_of(index):
-    m2 = jnp.floor((index + 0.5) * (1.0 / SIDE))
-    return m2, index - m2 * SIDE - TOP
+def pair_of(index, core):
+    tile = jnp.floor(index * 0.125)
+    place = index - 8.0 * tile
+    run = jnp.floor((tile + 0.5) * 0.2)
+    m2 = tile - 5.0 * run + 1.0 + 5.0 * core
+    last = run > 2.5
+    m2 = jnp.where(last, 0.0, m2)
+    run = jnp.where(last, core, run)
+    return m2, run_member(run, place)
+
+
+def run_member(run, place):
+    middle = jnp.where(place < 3, place + 8.0, -6.0 - place)
+    return jnp.where(run < 0.5, place, jnp.where(run < 1.5, middle, -1.0 - place))
+
+
+def place_of(m2, m3, core):
+    size = jnp.abs(m3)
+    outer = size > 8.5
+    middle = outer | (m3 == 8.0)
+    run = jnp.where(middle, 1.0, jnp.where(m3 < 0, 2.0, 0.0))
+    place = jnp.where(middle, jnp.where(m3 < 0, size - 6.0, m3 - 8.0), jnp.where(m3 < 0, size - 1.0, m3))
+    step = m2 - 1.0 - 5.0 * core
+    row = (run * 5.0 + step) * 8.0 + place
+    row = jnp.where((step >= 0) & (step < 5), row, -1.0)
+    return jnp.where(m2 == 0.0, jnp.where(run == core, 120.0 + place, -1.0), row)
 
 
 def split(value):
@@ -93,13 +98,46 @@
     return lax.dot_general(a, b, (((1,), (1,)), ((), ())), preferred_element_type=jnp.float32)
 
 
-def contract_kernel(table_ref, points_ref, waves_ref, out_ref, work_ref):
+def table_value(bead, contracted, beads):
+    turn = bead * (1.0 / beads) - contracted * (1.0 / CONTR)
+    total = 1.0 + math.sqrt(2.0) * cos_turns(turn * (CONTR // 2))
+    for mode in range(1, CONTR // 2):
+        total += 2.0 * cos_turns(turn * mode)
+    return total * (1.0 / beads)
+
+
+def contract_kernel(
+    beads_all,
+    points_from,
+    waves_from,
+    labels_from,
+    species_from,
+    out_ref,
+    charge_ref,
+    work_ref,
+    points_ref,
+    waves_ref,
+    labels_ref,
+    species_ref,
+    sems,
+):
+    copies_in = [
+        pltpu.make_async_copy(points_from.at[x], points_ref.at[x], sems.at[x]) for x in range(3)
+    ]
+    for i, (source, target) in enumerate(
+        ((waves_from, waves_ref), (labels_from, labels_ref), (species_from, species_ref))
+    ):
+        copies_in.append(pltpu.make_async_copy(source, target, sems.at[3 + i]))
+    for copy in copies_in:
+        copy.start()
     beads = points_ref.shape[1]
     tiles = points_ref.shape[2] // LANES
+    first = (lax.axis_index("bead") * beads).astype(jnp.float32)
     columns = [
-        jnp.broadcast_to(table_ref[:, b : b + 1], (CONTR, LANES)) for b in range(beads)
+        table_value(first + b, iota((CONTR, LANES), 0), beads_all) for b in range(beads)
     ]
     for x in range(3):
+        copies_in[x].wait()
         for t in range(tiles):
             block = points_ref[x, :, t * LANES : (t + 1) * LANES]
             total = columns[0] * jnp.broadcast_to(block[0:1], (CONTR, LANES))
@@ -107,6 +145,8 @@
                 total += columns[b] * jnp.broadcast_to(block[b : b + 1], (CONTR, LANES))
             row = (x * tiles + t) * CONTR
             work_ref[row : row + CONTR, :] = total
+    for copy in copies_in[3:]:
+        copy.wait()
     waves = waves_ref[...].astype(jnp.float32)
     used = 3 * tiles
     copies = out_ref.shape[0] // CONTR
@@ -115,13 +155,18 @@
         for c in range(copies):
             out_ref[j * copies + c, 0:used, :] = rows
             out_ref[j * copies + c, used : used + 3, :] = waves
+    labels = labels_ref[...]
+    charge = jnp.zeros(labels.shape, jnp.float32)
+    for kind in range(species_ref.shape[1]):
+        value = jnp.broadcast_to(species_ref[:, kind : kind + 1], labels.shape)
+        charge += jnp.where(labels == kind, value, 0.0)
+    charge_ref[...] = charge
 
 
 def structure_kernel(
     number_points,
     spots_ref,
-    labels_ref,
-    species_ref,
+    charge_ref,
     partial_ref,
     weights_ref,
     high_ref,
@@ -132,17 +177,13 @@
 ):
     core = lax.rem(lax.axis_index("bead"), 2).astype(jnp.float32)
     peers = spots_ref.shape[0]
-    tiles = labels_ref.shape[0]
+    tiles = charge_ref.shape[0]
     used = 3 * tiles
     spots = spots_ref[0, 0:used, :]
     for p in range(1, peers):
         spots += spots_ref[p, 0:used, :]
     spots = reduced(spots)
-    labels = labels_ref[...]
-    charge = jnp.zeros(labels.shape, jnp.float32)
-    for kind in range(species_ref.shape[0]):
-        charge += jnp.where(labels == kind, species_ref[kind], 0.0)
-    first = core * HALF
+    charge = charge_ref[...]
     grid_row = iota((2 * ROWS, LANES), 0)
     back = grid_row >= ROWS
     size = jnp.where(back, grid_row - ROWS, grid_row)
@@ -154,12 +195,15 @@
         m2 = spots_ref[p, used + 1 : used + 2, :]
         m3 = spots_ref[p, used + 2 : used + 3, :]
         sign = jnp.where(m2 < 0, -1.0, 1.0)
-        place = (m2 * sign) * SIDE + (m3 * sign) + TOP - first
-        place = jnp.where(place < HALF, place, -1.0)
+        fold = m2 * sign
+        m3 = m3 * sign
+        flip = jnp.where((fold == 0) & (m3 < 0), -1.0, 1.0)
+        sign = sign * flip
+        place = place_of(fold, m3 * flip, core)
         left = jnp.where(wanted == m1 * sign, 1.0, 0.0).astype(jnp.bfloat16)
         right = jnp.where(pair_row == place, 1.0, 0.0).astype(jnp.bfloat16)
         counts += dot_nt(left, right)
-    m2, m3 = pair_of(iota((2 * ROWS, LANES), 1) + first)
+    m2, m3 = pair_of(iota((2 * ROWS, LANES), 1), core)
     square = size * size + m2 * m2 + m3 * m3
     square = jnp.maximum(square, 1.0)
     weights_ref[...] = counts * (4.0 * jnp.exp(square * -0.01) / (square * number_points))
@@ -167,7 +211,6 @@
     sine = row >= ROWS
     m1 = jnp.where(sine, row - ROWS, row)
     phase = jnp.where(sine, 0.0, 0.25)
-    chunk = 32
     for t in range(tiles):
         lanes = slice(t * LANES, (t + 1) * LANES)
         x1 = spots[t : t + 1, :]
@@ -179,19 +222,29 @@
         high, low = split(plain)
         charged_ref[0 : 2 * ROWS, lanes] = high
         charged_ref[2 * ROWS :, lanes] = low
-    for r in range(0, LANES, chunk):
-        m2, m3 = pair_of(iota((chunk, LANES), 0) + (first + r))
-        for t in range(tiles):
-            lanes = slice(t * LANES, (t + 1) * LANES)
-            x2 = spots[tiles + t : tiles + t + 1, :]
-            x3 = spots[2 * tiles + t : 2 * tiles + t + 1, :]
-            cosine, sine = both_turns(m2 * x2 + m3 * x3)
-            high, low = split(cosine)
-            high_ref[r : r + chunk, lanes] = high
-            low_ref[r : r + chunk, lanes] = low
-            high, low = split(sine)
-            high_ref[LANES + r : LANES + r + chunk, lanes] = high
-            low_ref[LANES + r : LANES + r + chunk, lanes] = low
+    steps = 1.0 + 5.0 * core + iota((8, LANES), 0)
+    runs = [run_member(jnp.full((8, LANES), float(run)), iota((8, LANES), 0)) for run in range(3)]
+    for t in range(tiles):
+        lanes = slice(t * LANES, (t + 1) * LANES)
+        x2 = spots[tiles + t : tiles + t + 1, :]
+        x3 = spots[2 * tiles + t : 2 * tiles + t + 1, :]
+        cos2, sin2 = both_turns(steps * x2)
+        third = [both_turns(m * x3) for m in runs]
+        cosines, sines = [], []
+        for run in range(3):
+            cos3, sin3 = third[run]
+            for i in range(5):
+                c2 = jnp.broadcast_to(cos2[i : i + 1], (8, LANES))
+                s2 = jnp.broadcast_to(sin2[i : i + 1], (8, LANES))
+                cosines.append(c2 * cos3 - s2 * sin3)
+                sines.append(s2 * cos3 + c2 * sin3)
+        for values, index in ((cosines, 0), (sines, 1)):
+            values.append(jnp.where(core == 0.0, third[0][index], third[1][index]))
+            for r in range(0, 16, 2):
+                high, low = split(jnp.concatenate(values[r : r + 2], axis=0))
+                at = index * LANES + r * 8
+                high_ref[at : at + 16, lanes] = high
+                low_ref[at : at + 16, lanes] = low
     total = dot_nt(charged_ref[...], high_ref[...])
     total = (
         total[0 : 2 * ROWS]
@@ -219,7 +272,7 @@
     sc, ss = sin_row[:, :LANES], sin_row[:, LANES:]
     ahead_cos, ahead_sin = ahead * (cc - ss), ahead * (cs + sc)
     back_cos, back_sin = back * (cc + ss), back * (cs - sc)
-    m2, m3 = pair_of(iota((SENT, LANES), 1) + core * HALF)
+    m2, m3 = pair_of(iota((SENT, LANES), 1), core)
     coef_ref[...] = jnp.zeros_like(coef_ref)
     rows = (
         (ahead_cos + back_cos, ahead_sin + back_sin),
@@ -258,32 +311,47 @@
         out_ref[p, 0 : block.shape[0], :] = block
 
 
-def expand_kernel(table_ref, force_ref, out_ref, work_ref):
+def expand_kernel(beads_all, force_ref, out_to, work_ref, out_ref, sems):
     beads = out_ref.shape[1]
     tiles = out_ref.shape[2] // LANES
     used = 3 * tiles
     stride = work_ref.shape[0] // beads
     copies = force_ref.shape[0] // CONTR
-    parts = []
-    for j in range(CONTR):
-        part = force_ref[j * copies, 0:used, :]
-        for c in range(1, copies):
-            part += force_ref[j * copies + c, 0:used, :]
-        parts.append(part)
-    for b in range(beads):
-        total = parts[0] * table_ref[b, 0]
-        for j in range(1, CONTR):
-            total += parts[j] * table_ref[b, j]
-        work_ref[b * stride : b * stride + used, :] = total
-    for x in range(3):
-        for t in range(tiles):
+    first = (lax.axis_index("bead") * beads).astype(jnp.float32)
+    rows = iota((beads * CONTR, LANES), 0)
+    bead = jnp.floor((rows + 0.5) * (1.0 / CONTR))
+    table = table_value(first + bead, rows - CONTR * bead, beads_all)
+    done = 0
+    moves = []
+    for r in range(0, used, 8):
+        size = min(8, used - r)
+        parts = []
+        for j in range(CONTR):
+            part = force_ref[j * copies, r : r + size, :]
+            for c in range(1, copies):
+                part += force_ref[j * copies + c, r : r + size, :]
+            parts.append(part)
+        for b in range(beads):
+            at = b * CONTR
+            total = parts[0] * table[at : at + 1]
+            for j in range(1, CONTR):
+                total += parts[j] * table[at + j : at + j + 1]
+            work_ref[b * stride + r : b * stride + r + size, :] = total
+        for i in range(r, r + size):
+            x, t = divmod(i, tiles)
             out_ref[x, :, t * LANES : (t + 1) * LANES] = work_ref[
-                pl.ds(x * tiles + t, beads, stride=stride), :
+                pl.ds(i, beads, stride=stride), :
             ]
+        while done < 3 and (done + 1) * tiles <= r + size:
+            moves.append(pltpu.make_async_copy(out_ref.at[done], out_to.at[done], sems.at[done]))
+            moves[-1].start()
+            done += 1
+    for move in moves:
+        move.wait()
 
 
 VMEM = pl.BlockSpec(memory_space=pltpu.VMEM)
-SMEM = pl.BlockSpec(memory_space=pltpu.SMEM)
+HBM = pl.BlockSpec(memory_space=pltpu.HBM)
 PARAMS = pltpu.CompilerParams(vmem_limit_bytes=24 * 1024 * 1024)
 
 
@@ -299,18 +367,33 @@
     used = 3 * tiles
     sent = -(-(used + 3) // 8) * 8
     held = -(-used // 8) * 8
-    table = contraction_table(beads * bead_peers, CONTR)
-    blocks = jnp.asarray(table.reshape(CONTR, bead_peers, beads).transpose(1, 0, 2))
-    mine = lax.dynamic_index_in_dim(blocks, lax.axis_index("bead"), 0, keepdims=False)
-    portion = pl.pallas_call(
-        contract_kernel,
-        out_shape=shaped(bead_peers, sent, LANES),
-        in_specs=[VMEM] * 3,
-        out_specs=VMEM,
-        scratch_shapes=[pltpu.VMEM((used * CONTR, LANES), jnp.float32)],
+    beads_all = beads * bead_peers
+    portion, charge = pl.pallas_call(
+        functools.partial(contract_kernel, beads_all),
+        out_shape=[shaped(bead_peers, sent, LANES), shaped(tiles, LANES)],
+        in_specs=[HBM] * 4,
+        out_specs=[VMEM] * 2,
+        scratch_shapes=[
+            pltpu.VMEM((used * CONTR, LANES), jnp.float32),
+            pltpu.VMEM((3, beads, sites), jnp.float32),
+            pltpu.VMEM(waves.shape, jnp.int32),
+            pltpu.VMEM((tiles, LANES), jnp.int32),
+            pltpu.VMEM((1, species.shape[0]), jnp.float32),
+            pltpu.SemaphoreType.DMA((6,)),
+        ],
         compiler_params=PARAMS,
         name="contract",
-    )(mine, points.transpose(1, 0, 2), waves)
+    )(
+        *(
+            pltpu.with_memory_space_constraint(a, pltpu.HBM)
+            for a in (
+                points.transpose(1, 0, 2),
+                waves,
+                labels.reshape(tiles, LANES),
+                species[None, :],
+            )
+        )
+    )
     spots = lax.all_to_all(portion, "bead", 0, 0, tiled=True)
     partial, weights, high, low, plain, slope = pl.pallas_call(
         functools.partial(structure_kernel, float(sites * atom_peers)),
@@ -322,12 +405,12 @@
             shaped(2 * ROWS, sites),
             shaped(2 * ROWS, sites),
         ],
-        in_specs=[VMEM, VMEM, SMEM],
+        in_specs=[VMEM] * 2,
         out_specs=[VMEM] * 6,
         scratch_shapes=[pltpu.VMEM((4 * ROWS, sites), jnp.bfloat16)],
         compiler_params=PARAMS,
         name="structure",
-    )(spots, labels.reshape(tiles, LANES), species)
+    )(spots, charge)
     factors = lax.all_to_all(partial, "atom", 0, 0, tiled=True)
     force = pl.pallas_call(
         force_kernel,
@@ -343,14 +426,18 @@
     )(factors, weights, high, low, plain, slope)
     forces = lax.all_to_all(force, "bead", 0, 0, tiled=True)
     out = pl.pallas_call(
-        expand_kernel,
+        functools.partial(expand_kernel, beads_all),
         out_shape=shaped(3, beads, sites),
-        in_specs=[SMEM, VMEM],
-        out_specs=VMEM,
-        scratch_shapes=[pltpu.VMEM((beads * held, LANES), jnp.float32)],
+        in_specs=[VMEM],
+        out_specs=HBM,
+        scratch_shapes=[
+            pltpu.VMEM((beads * held, LANES), jnp.float32),
+            pltpu.VMEM((3, beads, sites), jnp.float32),
+            pltpu.SemaphoreType.DMA((3,)),
+        ],
         compiler_params=PARAMS,
         name="expand",
-    )(mine.T, forces)
+    )(forces)
     return out.transpose(1, 0, 2)
 
 

time: 51.1 us -> 47 us (0.920)
  blocking collectives: 28.6 us -> 43 us
  waiting for transfers between devices: 9.42 us -> 0 us
  starting transfers between devices: 5.14 us -> 0 us
  local copies, waits for them, and re-layouts: 2.34 us -> 0 us
  Pallas kernels: 5.26 us -> 3.72 us
    all_to_all x0 -> x1, blocking collectives: none -> 14.4 us  [local(): forces = lax.all_to_all(force, 'bead', 0, 0, tiled=True)]
    all_to_all x1 -> x0, waiting for transfers between devices: 9.42 us -> none  [local(): forces = lax.all_to_all(force, 'bead', 0, 0, tiled=True)]
    all_to_all x1 -> x0, starting transfers between devices: 5.14 us -> none  [local(): forces = lax.all_to_all(force, 'bead', 0, 0, tiled=True)]
    unnamed x8 -> x0, local copies, waits for them, and re-layouts: 1.57 us -> none
    pallas_call x1, Pallas kernels: 2.49 us -> 1.34 us  [local(): pl.pallas_call(functools.partial(structure_kernel, float(sites * atom_pee...]
    squeeze x2 -> x0, local copies, waits for them, and re-layouts: 0.77 us -> none  [local(): lax.dynamic_index_in_dim(blocks, lax.axis_index('bead'), 0, keepdims=False)]
    pallas_call x1, Pallas kernels: 1.21 us -> 0.47 us  [local(): pl.pallas_call(force_kernel, out_shape=shaped(bead_peers, held, LANES), i...]
  transfers between devices with their start and end apart: 1 -> 0, of which waited for: 1 -> 0; matrix products, arithmetic and copies ran while one was open for 0% -> 0% of each run, Pallas kernels for 0% -> 0%
where the time goes in v2:
time: 47 us; the launch traced here: 46.7 us
  blocking collectives  43 us (91%)
  Pallas kernels  3.72 us (8%)
    all_to_all x1, blocking collectives, local(): spots = lax.all_to_all(portion, 'bead', 0, 0, tiled=True)  17.7 us
    all_to_all x1, blocking collectives, local(): forces = lax.all_to_all(force, 'bead', 0, 0, tiled=True)  14.4 us
    all_to_all x1, blocking collectives, local(): factors = lax.all_to_all(partial, 'atom', 0, 0, tiled=True)  10.9 us
    pallas_call x1, Pallas kernels, local(): pl.pallas_call(functools.partial(structure_kernel, float(sites * atom_pee...  1.34 us
    pallas_call x1, Pallas kernels, local(): pl.pallas_call(functools.partial(contract_kernel, beads_all), out_shape=[...  1.04 us

profile of v2, /device:TPU:1, one launch (start us, length us, event | category | flops | bytes accessed | tf_op | source)
XLA Modules:
  0.0 46.7 jit_solution(16704182299555659715)
XLA Ops:
  0.0 1.0 %contract.1 = (f32[16,40,128]{2,1,0:T(8,128)S(1)}, f32[12,128]{1,0:T(8,128)S(1)}) custom-call(f32[3,8,1536]{2,1,0:T(8,128)} %bitcast.4, s32[3,128]{1,0:T(4,128)} %waves_from.1, s32[12,128]{1,0:T(8,128)} %bitcast.5, f32[1,4]{1,0:T(1,128)} %bitcast.6), custom_call_target="tpu_custom_call" | custom-call | tf_op jit(solution)/shard_map/contract/pallas_call | solution.py:371
  1.0 17.7 %all_to_all.15.spots_ref = f32[16,40,128]{2,1,0:T(8,128)S(1)} all-to-all(f32[16,40,128]{2,1,0:T(8,128)S(1)} %get-tuple-element.13), channel_id=1, replica_groups=mesh['bead'=16,'atom'=8] {'bead'}, dimensions={0} | all-to-all | bytes 655360 | tf_op jit(solution)/shard_map/all_to_all | solution.py:397
  18.8 1.3 %structure.1 = (f32[8,24,256]{2,1,0:T(8,128)S(1)}, f32[32,128]{1,0:T(8,128)S(1)}, bf16[256,1536]{1,0:T(8,128)(2,1)S(1)}, bf16[256,1536]{1,0:T(8,128)(2,1)S(1)}, ...) custom-call(f32[16,40,128]{2,1,0:T(8,128)S(1)} %all_to_all.15.spots_ref, f32[12,128]{1,0:T(8,128)S(1)} %get-tuple-element.14.charge_ref), custom_call_target="tpu_custom_call" | custom-call | tf_op jit(solution)/shard_map/structure/pallas_call | solution.py:398
  20.1 10.9 %all_to_all.16.partial_ref = f32[8,24,256]{2,1,0:T(8,128)S(1)} all-to-all(f32[8,24,256]{2,1,0:T(8,128)S(1)} %get-tuple-element.15), channel_id=1, replica_groups=mesh['bead'=16,'atom'=8] {'atom'}, dimensions={0} | all-to-all | bytes 393216 | tf_op jit(solution)/shard_map/all_to_all | solution.py:414
  31.0 0.5 %force.1 = f32[16,40,128]{2,1,0:T(8,128)S(1)} custom-call(f32[8,24,256]{2,1,0:T(8,128)S(1)} %all_to_all.16.partial_ref, f32[32,128]{1,0:T(8,128)S(1)} %get-tuple-element.16.weights_ref, bf16[256,1536]{1,0:T(8,128)(2,1)S(1)} %get-tuple-element.17.high_ref, bf16[256,1536]{1,0:T(8,128)(2,1)S(1)} %get-tuple-element.18.low_ref, ...), custom_call_target="tpu_custom_call" | custom-call | tf_op jit(solution)/shard_map/force/pallas_call | solution.py:415
  31.4 14.4 %all_to_all.17.force_ref = f32[16,40,128]{2,1,0:T(8,128)S(1)} all-to-all(f32[16,40,128]{2,1,0:T(8,128)S(1)} %force.1), channel_id=1, replica_groups=mesh['bead'=16,'atom'=8] {'bead'}, dimensions={0} | all-to-all | bytes 655360 | tf_op jit(solution)/shard_map/all_to_all | solution.py:427
  45.9 0.9 %expand.1 = f32[3,8,1536]{2,1,0:T(8,128)} custom-call(f32[16,40,128]{2,1,0:T(8,128)S(1)} %all_to_all.17.force_ref), custom_call_target="tpu_custom_call" | custom-call | tf_op jit(solution)/shard_map/expand/pallas_call | solution.py:428

commit v3 on v2

--- a/solution.py
+++ b/solution.py
@@ -163,6 +163,10 @@
     charge_ref[...] = charge
 
 
+def own_core():
+    return lax.rem(lax.axis_index("bead") + ORDERS["spots"] % 2, 2).astype(jnp.float32)
+
+
 def structure_kernel(
     number_points,
     spots_ref,
@@ -175,7 +179,7 @@
     slope_ref,
     charged_ref,
 ):
-    core = lax.rem(lax.axis_index("bead"), 2).astype(jnp.float32)
+    core = own_core()
     peers = spots_ref.shape[0]
     tiles = charge_ref.shape[0]
     used = 3 * tiles
@@ -259,7 +263,7 @@
 def force_kernel(
     partial_ref, weights_ref, high_ref, low_ref, plain_ref, slope_ref, out_ref, coef_ref, term_ref
 ):
-    core = lax.rem(lax.axis_index("bead"), 2).astype(jnp.float32)
+    core = own_core()
     tiles = plain_ref.shape[1] // LANES
     cos_row = partial_ref[0, 0:SENT, :]
     sin_row = partial_ref[0, SENT:, :]
@@ -327,9 +331,10 @@
         size = min(8, used - r)
         parts = []
         for j in range(CONTR):
-            part = force_ref[j * copies, r : r + size, :]
+            turn = ORDERS["spots"] ^ ORDERS["forces"]
+            part = force_ref[(j * copies) ^ turn, r : r + size, :]
             for c in range(1, copies):
-                part += force_ref[j * copies + c, r : r + size, :]
+                part += force_ref[(j * copies + c) ^ turn, r : r + size, :]
             parts.append(part)
         for b in range(beads):
             at = b * CONTR
@@ -353,6 +358,14 @@
 VMEM = pl.BlockSpec(memory_space=pltpu.VMEM)
 HBM = pl.BlockSpec(memory_space=pltpu.HBM)
 PARAMS = pltpu.CompilerParams(vmem_limit_bytes=24 * 1024 * 1024)
+
+
+ORDERS = {"spots": 14, "factors": 5, "forces": 15}
+
+
+def exchange(array, axis, key):
+    order = [i ^ ORDERS[key] for i in range(lax.axis_size(axis))]
+    return lax.all_to_all(array, axis, 0, 0, axis_index_groups=[order], tiled=True)
 
 
 def shaped(*shape, dtype=jnp.float32):
@@ -394,7 +407,7 @@
             )
         )
     )
-    spots = lax.all_to_all(portion, "bead", 0, 0, tiled=True)
+    spots = exchange(portion, "bead", "spots")
     partial, weights, high, low, plain, slope = pl.pallas_call(
         functools.partial(structure_kernel, float(sites * atom_peers)),
         out_shape=[
@@ -411,7 +424,7 @@
         compiler_params=PARAMS,
         name="structure",
     )(spots, charge)
-    factors = lax.all_to_all(partial, "atom", 0, 0, tiled=True)
+    factors = exchange(partial, "atom", "factors")
     force = pl.pallas_call(
         force_kernel,
         out_shape=shaped(bead_peers, held, LANES),
@@ -424,7 +437,7 @@
         compiler_params=PARAMS,
         name="force",
     )(factors, weights, high, low, plain, slope)
-    forces = lax.all_to_all(force, "bead", 0, 0, tiled=True)
+    forces = exchange(force, "bead", "forces")
     out = pl.pallas_call(
         functools.partial(expand_kernel, beads_all),
         out_shape=shaped(3, beads, sites),

time: 47 us -> 41.7 us (0.89)
  blocking collectives: 43 us -> 37.7 us
    all_to_all x3, blocking collectives: 43 us -> 37.7 us  [exchange(): lax.all_to_all(array, axis, 0, 0, axis_index_groups=[order], tiled=True)]
where the time goes in v3:
time: 41.7 us; the launch traced here: 41.5 us
  blocking collectives  37.7 us (90%)
  Pallas kernels  3.72 us (9%)
    all_to_all x3, blocking collectives, exchange(): lax.all_to_all(array, axis, 0, 0, axis_index_groups=[order], tiled=True)  37.7 us
    pallas_call x1, Pallas kernels, local(): pl.pallas_call(functools.partial(structure_kernel, float(sites * atom_pee...  1.34 us
    pallas_call x1, Pallas kernels, local(): pl.pallas_call(functools.partial(contract_kernel, beads_all), out_shape=[...  1.04 us
    pallas_call x1, Pallas kernels, local(): pl.pallas_call(functools.partial(expand_kernel, beads_all), out_shape=sha...  0.87 us

profile of v3, /device:TPU:1, one launch (start us, length us, event | category | flops | bytes accessed | tf_op | source)
XLA Modules:
  0.0 41.5 jit_solution(18437471247771627126)
XLA Ops:
  0.0 1.0 %contract.1 = (f32[16,40,128]{2,1,0:T(8,128)S(1)}, f32[12,128]{1,0:T(8,128)S(1)}) custom-call(f32[3,8,1536]{2,1,0:T(8,128)} %bitcast.4, s32[3,128]{1,0:T(4,128)} %waves_from.1, s32[12,128]{1,0:T(8,128)} %bitcast.5, f32[1,4]{1,0:T(1,128)} %bitcast.6), custom_call_target="tpu_custom_call" | custom-call | tf_op jit(solution)/shard_map/contract/pallas_call | solution.py:384
  1.0 14.4 %all_to_all.15.spots_ref = f32[16,40,128]{2,1,0:T(8,128)S(1)} all-to-all(f32[16,40,128]{2,1,0:T(8,128)S(1)} %get-tuple-element.13), channel_id=1, replica_groups={{112,120,96,104,80,88,64,72,48,56,32,40,16,24,0,8},{113,121,97,105,81,8..., dimensions={0} | all-to-all | bytes 655360 | tf_op jit(solution)/shard_map/all_to_all | solution.py:368
  15.4 1.3 %structure.1 = (f32[8,24,256]{2,1,0:T(8,128)S(1)}, f32[32,128]{1,0:T(8,128)S(1)}, bf16[256,1536]{1,0:T(8,128)(2,1)S(1)}, bf16[256,1536]{1,0:T(8,128)(2,1)S(1)}, ...) custom-call(f32[16,40,128]{2,1,0:T(8,128)S(1)} %all_to_all.15.spots_ref, f32[12,128]{1,0:T(8,128)S(1)} %get-tuple-element.14.charge_ref), custom_call_target="tpu_custom_call" | custom-call | tf_op jit(solution)/shard_map/structure/pallas_call | solution.py:411
  16.8 10.2 %all_to_all.16.partial_ref = f32[8,24,256]{2,1,0:T(8,128)S(1)} all-to-all(f32[8,24,256]{2,1,0:T(8,128)S(1)} %get-tuple-element.15), channel_id=1, replica_groups={{5,4,7,6,1,0,3,2},{13,12,15,14,9,8,11,10},{21,20,23,22,17,16,19,18},{29..., dimensions={0} | all-to-all | bytes 393216 | tf_op jit(solution)/shard_map/all_to_all | solution.py:368
  27.0 0.5 %force.1 = f32[16,40,128]{2,1,0:T(8,128)S(1)} custom-call(f32[8,24,256]{2,1,0:T(8,128)S(1)} %all_to_all.16.partial_ref, f32[32,128]{1,0:T(8,128)S(1)} %get-tuple-element.16.weights_ref, bf16[256,1536]{1,0:T(8,128)(2,1)S(1)} %get-tuple-element.17.high_ref, bf16[256,1536]{1,0:T(8,128)(2,1)S(1)} %get-tuple-element.18.low_ref, ...), custom_call_target="tpu_custom_call" | custom-call | tf_op jit(solution)/shard_map/force/pallas_call | solution.py:428
  27.5 13.1 %all_to_all.17.force_ref = f32[16,40,128]{2,1,0:T(8,128)S(1)} all-to-all(f32[16,40,128]{2,1,0:T(8,128)S(1)} %force.1), channel_id=1, replica_groups={{120,112,104,96,88,80,72,64,56,48,40,32,24,16,8,0},{121,113,105,97,89,8..., dimensions={0} | all-to-all | bytes 655360 | tf_op jit(solution)/shard_map/all_to_all | solution.py:368
  40.6 0.9 %expand.1 = f32[3,8,1536]{2,1,0:T(8,128)} custom-call(f32[16,40,128]{2,1,0:T(8,128)S(1)} %all_to_all.17.force_ref), custom_call_target="tpu_custom_call" | custom-call | tf_op jit(solution)/shard_map/expand/pallas_call | solution.py:441

commit v4 on v3

--- a/solution.py
+++ b/solution.py
@@ -72,16 +72,16 @@
 
 
 def run_member(run, place):
-    middle = jnp.where(place < 3, place + 8.0, -6.0 - place)
-    return jnp.where(run < 0.5, place, jnp.where(run < 1.5, middle, -1.0 - place))
+    middle = jnp.where(place < 0.5, 0.0, jnp.where(place < 2.5, place + 8.0, -6.0 - place))
+    return jnp.where(run < 0.5, place + 1.0, jnp.where(run < 1.5, middle, -1.0 - place))
 
 
 def place_of(m2, m3, core):
     size = jnp.abs(m3)
-    outer = size > 8.5
-    middle = outer | (m3 == 8.0)
+    middle = (size > 8.5) | (size < 0.5)
     run = jnp.where(middle, 1.0, jnp.where(m3 < 0, 2.0, 0.0))
-    place = jnp.where(middle, jnp.where(m3 < 0, size - 6.0, m3 - 8.0), jnp.where(m3 < 0, size - 1.0, m3))
+    inner = jnp.where(m3 < 0, size - 6.0, jnp.maximum(size - 8.0, 0.0))
+    place = jnp.where(middle, inner, size - 1.0)
     step = m2 - 1.0 - 5.0 * core
     row = (run * 5.0 + step) * 8.0 + place
     row = jnp.where((step >= 0) & (step < 5), row, -1.0)
@@ -114,6 +114,7 @@
     species_from,
     out_ref,
     charge_ref,
+    table_ref,
     work_ref,
     points_ref,
     waves_ref,
@@ -136,6 +137,8 @@
     columns = [
         table_value(first + b, iota((CONTR, LANES), 0), beads_all) for b in range(beads)
     ]
+    for b in range(beads):
+        table_ref[b * CONTR : (b + 1) * CONTR, :] = columns[b]
     for x in range(3):
         copies_in[x].wait()
         for t in range(tiles):
@@ -164,7 +167,10 @@
 
 
 def own_core():
-    return lax.rem(lax.axis_index("bead") + ORDERS["spots"] % 2, 2).astype(jnp.float32)
+    bits, first = ORDERS["spots"]
+    scale = 1 << bits[0]
+    bit = lax.rem(lax.div(lax.axis_index("bead"), scale), 2)
+    return (1 - bit if first & scale else bit).astype(jnp.float32)
 
 
 def structure_kernel(
@@ -176,7 +182,6 @@
     high_ref,
     low_ref,
     plain_ref,
-    slope_ref,
     charged_ref,
 ):
     core = own_core()
@@ -193,57 +198,51 @@
     size = jnp.where(back, grid_row - ROWS, grid_row)
     wanted = jnp.where(back, jnp.where(size > 0, -size, 1000.0), size)
     pair_row = iota((LANES, LANES), 0)
+    m1, m2, m3 = (spots_ref[:, used + x, :] for x in range(3))
+    sign = jnp.where(m2 < 0, -1.0, 1.0)
+    sign = jnp.where((m2 == 0) & (m3 < 0), -1.0, sign)
+    m1 = m1 * sign
+    place = place_of(m2 * sign, m3 * sign, core)
     counts = jnp.zeros((2 * ROWS, LANES), jnp.float32)
     for p in range(peers):
-        m1 = spots_ref[p, used : used + 1, :]
-        m2 = spots_ref[p, used + 1 : used + 2, :]
-        m3 = spots_ref[p, used + 2 : used + 3, :]
-        sign = jnp.where(m2 < 0, -1.0, 1.0)
-        fold = m2 * sign
-        m3 = m3 * sign
-        flip = jnp.where((fold == 0) & (m3 < 0), -1.0, 1.0)
-        sign = sign * flip
-        place = place_of(fold, m3 * flip, core)
-        left = jnp.where(wanted == m1 * sign, 1.0, 0.0).astype(jnp.bfloat16)
-        right = jnp.where(pair_row == place, 1.0, 0.0).astype(jnp.bfloat16)
+        left = jnp.where(wanted == m1[p : p + 1], 1.0, 0.0).astype(jnp.bfloat16)
+        right = jnp.where(pair_row == place[p : p + 1], 1.0, 0.0).astype(jnp.bfloat16)
         counts += dot_nt(left, right)
     m2, m3 = pair_of(iota((2 * ROWS, LANES), 1), core)
     square = size * size + m2 * m2 + m3 * m3
     square = jnp.maximum(square, 1.0)
     weights_ref[...] = counts * (4.0 * jnp.exp(square * -0.01) / (square * number_points))
-    row = iota((2 * ROWS, LANES), 0)
-    sine = row >= ROWS
-    m1 = jnp.where(sine, row - ROWS, row)
-    phase = jnp.where(sine, 0.0, 0.25)
+    size = iota((ROWS, LANES), 0)
+    steps = 1.0 + 5.0 * core + iota((8, LANES), 0)
+    place = iota((8, LANES), 0)
+    outer, middle = (run_member(jnp.full((8, LANES), run), place) for run in (0.0, 1.0))
     for t in range(tiles):
         lanes = slice(t * LANES, (t + 1) * LANES)
         x1 = spots[t : t + 1, :]
-        q = charge[t : t + 1, :]
-        angle = m1 * x1 + phase
-        plain = q * sin_turns(angle)
-        plain_ref[:, lanes] = plain
-        slope_ref[:, lanes] = (q * (-TWO_PI)) * m1 * sin_turns(angle + 0.25)
-        high, low = split(plain)
-        charged_ref[0 : 2 * ROWS, lanes] = high
-        charged_ref[2 * ROWS :, lanes] = low
-    steps = 1.0 + 5.0 * core + iota((8, LANES), 0)
-    runs = [run_member(jnp.full((8, LANES), float(run)), iota((8, LANES), 0)) for run in range(3)]
-    for t in range(tiles):
-        lanes = slice(t * LANES, (t + 1) * LANES)
         x2 = spots[tiles + t : tiles + t + 1, :]
         x3 = spots[2 * tiles + t : 2 * tiles + t + 1, :]
+        q = charge[t : t + 1, :]
+        for index, value in enumerate(both_turns(size * x1)):
+            value = q * value
+            at = index * ROWS
+            plain_ref[at : at + ROWS, lanes] = value
+            high, low = split(value)
+            charged_ref[at : at + ROWS, lanes] = high
+            charged_ref[2 * ROWS + at : 3 * ROWS + at, lanes] = low
         cos2, sin2 = both_turns(steps * x2)
-        third = [both_turns(m * x3) for m in runs]
-        cosines, sines = [], []
-        for run in range(3):
-            cos3, sin3 = third[run]
-            for i in range(5):
-                c2 = jnp.broadcast_to(cos2[i : i + 1], (8, LANES))
-                s2 = jnp.broadcast_to(sin2[i : i + 1], (8, LANES))
-                cosines.append(c2 * cos3 - s2 * sin3)
-                sines.append(s2 * cos3 + c2 * sin3)
-        for values, index in ((cosines, 0), (sines, 1)):
-            values.append(jnp.where(core == 0.0, third[0][index], third[1][index]))
+        cos3, sin3 = both_turns(outer * x3)
+        cos4, sin4 = both_turns(middle * x3)
+        cosines, sines = [None] * 15, [None] * 15
+        for i in range(5):
+            c2 = jnp.broadcast_to(cos2[i : i + 1], (8, LANES))
+            s2 = jnp.broadcast_to(sin2[i : i + 1], (8, LANES))
+            cc, ss, sc, cs = c2 * cos3, s2 * sin3, s2 * cos3, c2 * sin3
+            cosines[i], sines[i] = cc - ss, sc + cs
+            cosines[5 + i], sines[5 + i] = c2 * cos4 - s2 * sin4, s2 * cos4 + c2 * sin4
+            cosines[10 + i], sines[10 + i] = cc + ss, sc - cs
+        cosines.append(jnp.where(core == 0.0, cos3, cos4))
+        sines.append(jnp.where(core == 0.0, sin3, sin4))
+        for index, values in enumerate((cosines, sines)):
             for r in range(0, 16, 2):
                 high, low = split(jnp.concatenate(values[r : r + 2], axis=0))
                 at = index * LANES + r * 8
@@ -261,7 +260,7 @@
 
 
 def force_kernel(
-    partial_ref, weights_ref, high_ref, low_ref, plain_ref, slope_ref, out_ref, coef_ref, term_ref
+    partial_ref, weights_ref, high_ref, low_ref, plain_ref, out_ref, coef_ref, term_ref
 ):
     core = own_core()
     tiles = plain_ref.shape[1] // LANES
@@ -282,10 +281,12 @@
         (ahead_cos + back_cos, ahead_sin + back_sin),
         (ahead_sin - back_sin, back_cos - ahead_cos),
     )
+    m1 = TWO_PI * iota((SENT, LANES), 0)
     for kind, (on_cos, on_sin) in enumerate(rows):
-        at = kind * ROWS
-        coef_ref[at : at + SENT, :LANES] = on_cos
-        coef_ref[at : at + SENT, LANES:] = on_sin
+        at = (1 - kind) * ROWS
+        along = m1 if kind == 0 else -m1
+        coef_ref[at : at + SENT, :LANES] = along * on_cos
+        coef_ref[at : at + SENT, LANES:] = along * on_sin
         for axis, m in enumerate((m2, m3)):
             at = kind * ROWS + 2 * ROWS * (axis + 1)
             coef_ref[at : at + SENT, :LANES] = (-TWO_PI) * m * on_sin
@@ -300,12 +301,9 @@
         far = jnp.dot(high, low_ref[:, lanes], preferred_element_type=jnp.float32)
         term = near[:size] + near[size:] + far
         plain = plain_ref[:, lanes]
-        values = [term[0 : 2 * ROWS] * slope_ref[:, lanes]]
-        for axis in range(2):
-            at = 2 * ROWS * (axis + 1)
-            values.append(term[at : at + 2 * ROWS] * plain)
-        for x, value in enumerate(values):
-            total = jnp.sum(value, axis=0, keepdims=True)
+        for x in range(3):
+            at = 2 * ROWS * x
+            total = jnp.sum(term[at : at + 2 * ROWS] * plain, axis=0, keepdims=True)
             for i in range(2):
                 term_ref[x * tiles + t + i : x * tiles + t + i + 1, :] = total[
                     :, i * LANES : (i + 1) * LANES
@@ -315,26 +313,24 @@
         out_ref[p, 0 : block.shape[0], :] = block
 
 
-def expand_kernel(beads_all, force_ref, out_to, work_ref, out_ref, sems):
+def expand_kernel(table_ref, force_ref, out_to, work_ref, out_ref, sems):
     beads = out_ref.shape[1]
     tiles = out_ref.shape[2] // LANES
     used = 3 * tiles
     stride = work_ref.shape[0] // beads
     copies = force_ref.shape[0] // CONTR
-    first = (lax.axis_index("bead") * beads).astype(jnp.float32)
-    rows = iota((beads * CONTR, LANES), 0)
-    bead = jnp.floor((rows + 0.5) * (1.0 / CONTR))
-    table = table_value(first + bead, rows - CONTR * bead, beads_all)
+    table = table_ref[...]
+    arrivals = members("forces")
+    senders = [arrivals.index(member) for member in members("spots")]
     done = 0
     moves = []
     for r in range(0, used, 8):
         size = min(8, used - r)
         parts = []
         for j in range(CONTR):
-            turn = ORDERS["spots"] ^ ORDERS["forces"]
-            part = force_ref[(j * copies) ^ turn, r : r + size, :]
+            part = force_ref[senders[j * copies], r : r + size, :]
             for c in range(1, copies):
-                part += force_ref[(j * copies + c) ^ turn, r : r + size, :]
+                part += force_ref[senders[j * copies + c], r : r + size, :]
             parts.append(part)
         for b in range(beads):
             at = b * CONTR
@@ -360,12 +356,25 @@
 PARAMS = pltpu.CompilerParams(vmem_limit_bytes=24 * 1024 * 1024)
 
 
-ORDERS = {"spots": 14, "factors": 5, "forces": 15}
+ORDERS = {
+    "spots": ((0, 1, 2, 3), 14),
+    "factors": ((0, 1, 2), 5),
+    "forces": ((0, 1, 2, 3), 15),
+}
+
+
+def members(key):
+    bits, first = ORDERS[key]
+    return [
+        sum((place >> i & 1) << bit for i, bit in enumerate(bits)) ^ first
+        for place in range(1 << len(bits))
+    ]
 
 
 def exchange(array, axis, key):
-    order = [i ^ ORDERS[key] for i in range(lax.axis_size(axis))]
-    return lax.all_to_all(array, axis, 0, 0, axis_index_groups=[order], tiled=True)
+    return lax.all_to_all(
+        array, axis, 0, 0, axis_index_groups=[members(key)], tiled=True
+    )
 
 
 def shaped(*shape, dtype=jnp.float32):
@@ -381,11 +390,15 @@
     sent = -(-(used + 3) // 8) * 8
     held = -(-used // 8) * 8
     beads_all = beads * bead_peers
-    portion, charge = pl.pallas_call(
+    portion, charge, table = pl.pallas_call(
         functools.partial(contract_kernel, beads_all),
-        out_shape=[shaped(bead_peers, sent, LANES), shaped(tiles, LANES)],
+        out_shape=[
+            shaped(bead_peers, sent, LANES),
+            shaped(tiles, LANES),
+            shaped(beads * CONTR, LANES),
+        ],
         in_specs=[HBM] * 4,
-        out_specs=[VMEM] * 2,
+        out_specs=[VMEM] * 3,
         scratch_shapes=[
             pltpu.VMEM((used * CONTR, LANES), jnp.float32),
             pltpu.VMEM((3, beads, sites), jnp.float32),
@@ -408,7 +421,7 @@
         )
     )
     spots = exchange(portion, "bead", "spots")
-    partial, weights, high, low, plain, slope = pl.pallas_call(
+    partial, weights, high, low, plain = pl.pallas_call(
         functools.partial(structure_kernel, float(sites * atom_peers)),
         out_shape=[
             shaped(atom_peers, 2 * SENT, 2 * LANES),
@@ -416,10 +429,9 @@
             shaped(2 * LANES, sites, dtype=jnp.bfloat16),
             shaped(2 * LANES, sites, dtype=jnp.bfloat16),
             shaped(2 * ROWS, sites),
-            shaped(2 * ROWS, sites),
         ],
         in_specs=[VMEM] * 2,
-        out_specs=[VMEM] * 6,
+        out_specs=[VMEM] * 5,
         scratch_shapes=[pltpu.VMEM((4 * ROWS, sites), jnp.bfloat16)],
         compiler_params=PARAMS,
         name="structure",
@@ -428,7 +440,7 @@
     force = pl.pallas_call(
         force_kernel,
         out_shape=shaped(bead_peers, held, LANES),
-        in_specs=[VMEM] * 6,
+        in_specs=[VMEM] * 5,
         out_specs=VMEM,
         scratch_shapes=[
             pltpu.VMEM((6 * ROWS, 2 * LANES), jnp.float32),
@@ -436,12 +448,12 @@
         ],
         compiler_params=PARAMS,
         name="force",
-    )(factors, weights, high, low, plain, slope)
+    )(factors, weights, high, low, plain)
     forces = exchange(force, "bead", "forces")
     out = pl.pallas_call(
-        functools.partial(expand_kernel, beads_all),
+        expand_kernel,
         out_shape=shaped(3, beads, sites),
-        in_specs=[VMEM],
+        in_specs=[VMEM] * 2,
         out_specs=HBM,
         scratch_shapes=[
             pltpu.VMEM((beads * held, LANES), jnp.float32),
@@ -450,7 +462,7 @@
         ],
         compiler_params=PARAMS,
         name="expand",
-    )(forces)
+    )(table, forces)
     return out.transpose(1, 0, 2)
 
 

time: 41.7 us -> 41.4 us (level)
  no operation moved by 1% of the time
where the time goes in v4:
time: 41.4 us; the launch traced here: 41.1 us
  blocking collectives  37.7 us (91%)
  Pallas kernels  3.35 us (8%)
    all_to_all x3, blocking collectives, exchange(): lax.all_to_all(array, axis, 0, 0, axis_index_groups=[members(key)], tiled...  37.7 us
    pallas_call x1, Pallas kernels, local(): pl.pallas_call(functools.partial(structure_kernel, float(sites * atom_pee...  1.08 us
    pallas_call x1, Pallas kernels, local(): pl.pallas_call(functools.partial(contract_kernel, beads_all), out_shape=[...  1.04 us

profile of v4, /device:TPU:1, one launch (start us, length us, event | category | flops | bytes accessed | tf_op | source)
XLA Modules:
  0.0 41.1 jit_solution(17727702811658819311)
XLA Ops:
  0.0 1.0 %contract.1 = (f32[16,40,128]{2,1,0:T(8,128)S(1)}, f32[12,128]{1,0:T(8,128)S(1)}, f32[64,128]{1,0:T(8,128)S(1)}) custom-call(f32[3,8,1536]{2,1,0:T(8,128)} %bitcast.4, s32[3,128]{1,0:T(4,128)} %waves_from.1, s32[12,128]{1,0:T(8,128)} %bitcast.5, f32[1,4]{1,0:T(1,128)} %bitcast.6), custom_call_target="tpu_custom_call" | custom-call | tf_op jit(solution)/shard_map/contract/pallas_call | solution.py:393
  1.0 14.4 %all_to_all.15.spots_ref = f32[16,40,128]{2,1,0:T(8,128)S(1)} all-to-all(f32[16,40,128]{2,1,0:T(8,128)S(1)} %get-tuple-element.14), channel_id=1, replica_groups={{112,120,96,104,80,88,64,72,48,56,32,40,16,24,0,8},{113,121,97,105,81,8..., dimensions={0} | all-to-all | bytes 655360 | tf_op jit(solution)/shard_map/all_to_all | solution.py:375
  15.4 1.1 %structure.1 = (f32[8,24,256]{2,1,0:T(8,128)S(1)}, f32[32,128]{1,0:T(8,128)S(1)}, bf16[256,1536]{1,0:T(8,128)(2,1)S(1)}, bf16[256,1536]{1,0:T(8,128)(2,1)S(1)}, f32[32,1536]{1,0:T(8,128)S(1)}) custom-call(f32[16,40,128]{2,1,0:T(8,128)S(1)} %all_to_all.15.spots_ref, f32[12,128]{1,0:T(8,128)S(1)} %get-tuple-element.15.charge_ref), custom_call_target="tpu_custom_call" | custom-call | tf_op jit(solution)/shard_map/structure/pallas_call | solution.py:424
  16.5 10.2 %all_to_all.16.partial_ref = f32[8,24,256]{2,1,0:T(8,128)S(1)} all-to-all(f32[8,24,256]{2,1,0:T(8,128)S(1)} %get-tuple-element.16), channel_id=1, replica_groups={{5,4,7,6,1,0,3,2},{13,12,15,14,9,8,11,10},{21,20,23,22,17,16,19,18},{29..., dimensions={0} | all-to-all | bytes 393216 | tf_op jit(solution)/shard_map/all_to_all | solution.py:375
  26.7 0.5 %force.1 = f32[16,40,128]{2,1,0:T(8,128)S(1)} custom-call(f32[8,24,256]{2,1,0:T(8,128)S(1)} %all_to_all.16.partial_ref, f32[32,128]{1,0:T(8,128)S(1)} %get-tuple-element.17.weights_ref, bf16[256,1536]{1,0:T(8,128)(2,1)S(1)} %get-tuple-element.18.high_ref, bf16[256,1536]{1,0:T(8,128)(2,1)S(1)} %get-tuple-element.19.low_ref, ...), custom_call_target="tpu_custom_call" | custom-call | tf_op jit(solution)/shard_map/force/pallas_call | solution.py:440
  27.2 13.1 %all_to_all.17.force_ref = f32[16,40,128]{2,1,0:T(8,128)S(1)} all-to-all(f32[16,40,128]{2,1,0:T(8,128)S(1)} %force.1), channel_id=1, replica_groups={{120,112,104,96,88,80,72,64,56,48,40,32,24,16,8,0},{121,113,105,97,89,8..., dimensions={0} | all-to-all | bytes 655360 | tf_op jit(solution)/shard_map/all_to_all | solution.py:375
  40.3 0.8 %expand.1 = f32[3,8,1536]{2,1,0:T(8,128)} custom-call(f32[64,128]{1,0:T(8,128)S(1)} %get-tuple-element.13.table_ref, f32[16,40,128]{2,1,0:T(8,128)S(1)} %all_to_all.17.force_ref), custom_call_target="tpu_custom_call" | custom-call | tf_op jit(solution)/shard_map/expand/pallas_call | solution.py:453

commit v5 on v4

--- a/solution.py
+++ b/solution.py
@@ -112,7 +112,8 @@
     waves_from,
     labels_from,
     species_from,
-    out_ref,
+    kept_ref,
+    given_ref,
     charge_ref,
     table_ref,
     work_ref,
@@ -133,9 +134,11 @@
         copy.start()
     beads = points_ref.shape[1]
     tiles = points_ref.shape[2] // LANES
-    first = (lax.axis_index("bead") * beads).astype(jnp.float32)
+    bead_index = lax.axis_index("bead")
+    first = (bead_index * beads).astype(jnp.float32)
+    start = (lax.rem(bead_index, 2) * (CONTR // 2)).astype(jnp.float32)
     columns = [
-        table_value(first + b, iota((CONTR, LANES), 0), beads_all) for b in range(beads)
+        table_value(first + b, iota((CONTR, LANES), 0) + start, beads_all) for b in range(beads)
     ]
     for b in range(beads):
         table_ref[b * CONTR : (b + 1) * CONTR, :] = columns[b]
@@ -148,16 +151,16 @@
                 total += columns[b] * jnp.broadcast_to(block[b : b + 1], (CONTR, LANES))
             row = (x * tiles + t) * CONTR
             work_ref[row : row + CONTR, :] = total
+    used = 3 * tiles
+    half = CONTR // 2
+    for target, begin in ((given_ref, half), (kept_ref, 0)):
+        for j in range(half):
+            target[j, 0:used, :] = work_ref[pl.ds(begin + j, used, stride=CONTR), :]
     for copy in copies_in[3:]:
         copy.wait()
     waves = waves_ref[...].astype(jnp.float32)
-    used = 3 * tiles
-    copies = out_ref.shape[0] // CONTR
-    for j in range(CONTR):
-        rows = work_ref[pl.ds(j, used, stride=CONTR), :]
-        for c in range(copies):
-            out_ref[j * copies + c, 0:used, :] = rows
-            out_ref[j * copies + c, used : used + 3, :] = waves
+    for target in (given_ref, kept_ref):
+        target[0, used : used + 3, :] = waves
     labels = labels_ref[...]
     charge = jnp.zeros(labels.shape, jnp.float32)
     for kind in range(species_ref.shape[1]):
@@ -166,11 +169,22 @@
     charge_ref[...] = charge
 
 
-def own_core():
-    bits, first = ORDERS["spots"]
-    scale = 1 << bits[0]
-    bit = lax.rem(lax.div(lax.axis_index("bead"), scale), 2)
-    return (1 - bit if first & scale else bit).astype(jnp.float32)
+def pair_sum_kernel(used, kept_ref, taken_ref, out_ref):
+    copies = out_ref.shape[0] // kept_ref.shape[0]
+    kept_waves = kept_ref[0, used : used + 3, :]
+    taken_waves = taken_ref[0, used : used + 3, :]
+    for j in range(kept_ref.shape[0]):
+        total = kept_ref[j, 0:used, :] + taken_ref[j, 0:used, :]
+        for c in range(copies):
+            out_ref[j * copies + c, 0:used, :] = total
+            out_ref[j * copies + c, used : used + 3, :] = kept_waves
+            out_ref[j * copies + c, used + 3 : used + 6, :] = taken_waves
+
+
+def own_half():
+    first = ORDERS["spots"]
+    bit = lax.rem(lax.div(lax.axis_index("bead"), 2) + first % 2, 2)
+    return bit.astype(jnp.float32)
 
 
 def structure_kernel(
@@ -184,7 +198,7 @@
     plain_ref,
     charged_ref,
 ):
-    core = own_core()
+    half = own_half()
     peers = spots_ref.shape[0]
     tiles = charge_ref.shape[0]
     used = 3 * tiles
@@ -198,22 +212,25 @@
     size = jnp.where(back, grid_row - ROWS, grid_row)
     wanted = jnp.where(back, jnp.where(size > 0, -size, 1000.0), size)
     pair_row = iota((LANES, LANES), 0)
-    m1, m2, m3 = (spots_ref[:, used + x, :] for x in range(3))
+    m1, m2, m3 = (
+        jnp.concatenate([spots_ref[:, used + x, :], spots_ref[:, used + 3 + x, :]], axis=0)
+        for x in range(3)
+    )
     sign = jnp.where(m2 < 0, -1.0, 1.0)
     sign = jnp.where((m2 == 0) & (m3 < 0), -1.0, sign)
     m1 = m1 * sign
-    place = place_of(m2 * sign, m3 * sign, core)
+    place = place_of(m2 * sign, m3 * sign, half)
     counts = jnp.zeros((2 * ROWS, LANES), jnp.float32)
-    for p in range(peers):
+    for p in range(2 * peers):
         left = jnp.where(wanted == m1[p : p + 1], 1.0, 0.0).astype(jnp.bfloat16)
         right = jnp.where(pair_row == place[p : p + 1], 1.0, 0.0).astype(jnp.bfloat16)
         counts += dot_nt(left, right)
-    m2, m3 = pair_of(iota((2 * ROWS, LANES), 1), core)
+    m2, m3 = pair_of(iota((2 * ROWS, LANES), 1), half)
     square = size * size + m2 * m2 + m3 * m3
     square = jnp.maximum(square, 1.0)
     weights_ref[...] = counts * (4.0 * jnp.exp(square * -0.01) / (square * number_points))
     size = iota((ROWS, LANES), 0)
-    steps = 1.0 + 5.0 * core + iota((8, LANES), 0)
+    steps = 1.0 + 5.0 * half + iota((8, LANES), 0)
     place = iota((8, LANES), 0)
     outer, middle = (run_member(jnp.full((8, LANES), run), place) for run in (0.0, 1.0))
     for t in range(tiles):
@@ -240,8 +257,8 @@
             cosines[i], sines[i] = cc - ss, sc + cs
             cosines[5 + i], sines[5 + i] = c2 * cos4 - s2 * sin4, s2 * cos4 + c2 * sin4
             cosines[10 + i], sines[10 + i] = cc + ss, sc - cs
-        cosines.append(jnp.where(core == 0.0, cos3, cos4))
-        sines.append(jnp.where(core == 0.0, sin3, sin4))
+        cosines.append(jnp.where(half == 0.0, cos3, cos4))
+        sines.append(jnp.where(half == 0.0, sin3, sin4))
         for index, values in enumerate((cosines, sines)):
             for r in range(0, 16, 2):
                 high, low = split(jnp.concatenate(values[r : r + 2], axis=0))
@@ -262,7 +279,7 @@
 def force_kernel(
     partial_ref, weights_ref, high_ref, low_ref, plain_ref, out_ref, coef_ref, term_ref
 ):
-    core = own_core()
+    half = own_half()
     tiles = plain_ref.shape[1] // LANES
     cos_row = partial_ref[0, 0:SENT, :]
     sin_row = partial_ref[0, SENT:, :]
@@ -275,7 +292,7 @@
     sc, ss = sin_row[:, :LANES], sin_row[:, LANES:]
     ahead_cos, ahead_sin = ahead * (cc - ss), ahead * (cs + sc)
     back_cos, back_sin = back * (cc + ss), back * (cs - sc)
-    m2, m3 = pair_of(iota((SENT, LANES), 1), core)
+    m2, m3 = pair_of(iota((SENT, LANES), 1), half)
     coef_ref[...] = jnp.zeros_like(coef_ref)
     rows = (
         (ahead_cos + back_cos, ahead_sin + back_sin),
@@ -313,25 +330,30 @@
         out_ref[p, 0 : block.shape[0], :] = block
 
 
-def expand_kernel(table_ref, force_ref, out_to, work_ref, out_ref, sems):
+def gather_kernel(used, force_ref, out_ref):
+    arrivals = members("forces")
+    senders = [arrivals.index(member) for member in members("spots")]
+    copies = force_ref.shape[0] // out_ref.shape[0]
+    for j in range(out_ref.shape[0]):
+        total = force_ref[senders[j * copies], 0:used, :]
+        for c in range(1, copies):
+            total += force_ref[senders[j * copies + c], 0:used, :]
+        out_ref[j, 0:used, :] = total
+
+
+def expand_kernel(table_ref, kept_ref, taken_ref, out_to, work_ref, out_ref, sems):
     beads = out_ref.shape[1]
     tiles = out_ref.shape[2] // LANES
     used = 3 * tiles
     stride = work_ref.shape[0] // beads
-    copies = force_ref.shape[0] // CONTR
     table = table_ref[...]
-    arrivals = members("forces")
-    senders = [arrivals.index(member) for member in members("spots")]
     done = 0
     moves = []
     for r in range(0, used, 8):
         size = min(8, used - r)
-        parts = []
-        for j in range(CONTR):
-            part = force_ref[senders[j * copies], r : r + size, :]
-            for c in range(1, copies):
-                part += force_ref[senders[j * copies + c], r : r + size, :]
-            parts.append(part)
+        parts = [
+            source[j, r : r + size, :] for source in (kept_ref, taken_ref) for j in range(CONTR // 2)
+        ]
         for b in range(beads):
             at = b * CONTR
             total = parts[0] * table[at : at + 1]
@@ -356,25 +378,21 @@
 PARAMS = pltpu.CompilerParams(vmem_limit_bytes=24 * 1024 * 1024)
 
 
-ORDERS = {
-    "spots": ((0, 1, 2, 3), 14),
-    "factors": ((0, 1, 2), 5),
-    "forces": ((0, 1, 2, 3), 15),
-}
+ORDERS = {"spots": 5, "factors": 5, "forces": 5}
 
 
 def members(key):
-    bits, first = ORDERS[key]
-    return [
-        sum((place >> i & 1) << bit for i, bit in enumerate(bits)) ^ first
-        for place in range(1 << len(bits))
-    ]
-
-
-def exchange(array, axis, key):
-    return lax.all_to_all(
-        array, axis, 0, 0, axis_index_groups=[members(key)], tiled=True
-    )
+    return [place ^ ORDERS[key] for place in range(8)]
+
+
+def between_chips(array, key):
+    groups = [[2 * chip + core for chip in members(key)] for core in range(2)]
+    return lax.all_to_all(array, "bead", 0, 0, axis_index_groups=groups, tiled=True)
+
+
+def between_cores(array):
+    peers = lax.axis_size("bead")
+    return lax.ppermute(array, "bead", [(i, i ^ 1) for i in range(peers)])
 
 
 def shaped(*shape, dtype=jnp.float32):
@@ -387,18 +405,22 @@
     atom_peers = lax.axis_size("atom")
     tiles = sites // LANES
     used = 3 * tiles
-    sent = -(-(used + 3) // 8) * 8
+    rows = -(-(used + 3) // 8) * 8
+    sent = -(-(used + 6) // 8) * 8
     held = -(-used // 8) * 8
+    half = CONTR // 2
+    chips = bead_peers // 2
     beads_all = beads * bead_peers
-    portion, charge, table = pl.pallas_call(
+    kept, given, charge, table = pl.pallas_call(
         functools.partial(contract_kernel, beads_all),
         out_shape=[
-            shaped(bead_peers, sent, LANES),
+            shaped(half, rows, LANES),
+            shaped(half, rows, LANES),
             shaped(tiles, LANES),
             shaped(beads * CONTR, LANES),
         ],
         in_specs=[HBM] * 4,
-        out_specs=[VMEM] * 3,
+        out_specs=[VMEM] * 4,
         scratch_shapes=[
             pltpu.VMEM((used * CONTR, LANES), jnp.float32),
             pltpu.VMEM((3, beads, sites), jnp.float32),
@@ -420,7 +442,15 @@
             )
         )
     )
-    spots = exchange(portion, "bead", "spots")
+    portion = pl.pallas_call(
+        functools.partial(pair_sum_kernel, used),
+        out_shape=shaped(chips, sent, LANES),
+        in_specs=[VMEM] * 2,
+        out_specs=VMEM,
+        compiler_params=PARAMS,
+        name="pair_sum",
+    )(kept, between_cores(given))
+    spots = between_chips(portion, "spots")
     partial, weights, high, low, plain = pl.pallas_call(
         functools.partial(structure_kernel, float(sites * atom_peers)),
         out_shape=[
@@ -436,10 +466,12 @@
         compiler_params=PARAMS,
         name="structure",
     )(spots, charge)
-    factors = exchange(partial, "atom", "factors")
+    factors = lax.all_to_all(
+        partial, "atom", 0, 0, axis_index_groups=[members("factors")], tiled=True
+    )
     force = pl.pallas_call(
         force_kernel,
-        out_shape=shaped(bead_peers, held, LANES),
+        out_shape=shaped(chips, held, LANES),
         in_specs=[VMEM] * 5,
         out_specs=VMEM,
         scratch_shapes=[
@@ -449,11 +481,18 @@
         compiler_params=PARAMS,
         name="force",
     )(factors, weights, high, low, plain)
-    forces = exchange(force, "bead", "forces")
+    gathered = pl.pallas_call(
+        functools.partial(gather_kernel, used),
+        out_shape=shaped(half, held, LANES),
+        in_specs=[VMEM],
+        out_specs=VMEM,
+        compiler_params=PARAMS,
+        name="gather",
+    )(between_chips(force, "forces"))
     out = pl.pallas_call(
         expand_kernel,
         out_shape=shaped(3, beads, sites),
-        in_specs=[VMEM] * 2,
+        in_specs=[VMEM] * 3,
         out_specs=HBM,
         scratch_shapes=[
             pltpu.VMEM((beads * held, LANES), jnp.float32),
@@ -462,7 +501,7 @@
         ],
         compiler_params=PARAMS,
         name="expand",
-    )(table, forces)
+    )(table, gathered, between_cores(gathered))
     return out.transpose(1, 0, 2)
 
 

time: 41.4 us -> 40.6 us (0.981)
  blocking collectives: 37.7 us -> 30 us
  starting transfers between devices: 0 us -> 5.13 us
  waiting for transfers between devices: 0 us -> 1.85 us
    all_to_all x3, blocking collectives: 37.7 us -> 30 us  [the longest x2 20.3 us: between_chips(): lax.all_to_all(array, 'bead', 0, 0, axis_index_groups=groups, tiled=True)]
    ppermute x0 -> x2, starting transfers between devices: none -> 5.13 us  [between_cores(): return lax.ppermute(array, 'bead', [(i, i ^ 1) for i in range(peers)])]
    ppermute x0 -> x2, waiting for transfers between devices: none -> 1.85 us  [between_cores(): return lax.ppermute(array, 'bead', [(i, i ^ 1) for i in range(peers)])]
  transfers between devices with their start and end apart: 0 -> 2, of which waited for: 0 -> 2; matrix products, arithmetic and copies ran while one was open for 0% -> 0% of each run, Pallas kernels for 0% -> 0%
where the time goes in v5:
time: 40.6 us; the launch traced here: 40.4 us
  blocking collectives  30 us (74%)
  starting transfers between devices  5.13 us (13%)
  Pallas kernels  3.34 us (8%)
  waiting for transfers between devices  1.85 us (5%)
    all_to_all x2, blocking collectives, between_chips(): lax.all_to_all(array, 'bead', 0, 0, axis_index_groups=groups, tiled=True)  20.3 us
    all_to_all x1, blocking collectives, local(): lax.all_to_all(partial, 'atom', 0, 0, axis_index_groups=[members('factors...  9.7 us
    ppermute x2, starting transfers between devices, between_cores(): return lax.ppermute(array, 'bead', [(i, i ^ 1) for i in range(peers)])  5.13 us
    ppermute x2, waiting for transfers between devices, between_cores(): return lax.ppermute(array, 'bead', [(i, i ^ 1) for i in range(peers)])  1.85 us
    pallas_call x1, Pallas kernels, local(): pl.pallas_call(functools.partial(structure_kernel, float(sites * atom_pee...  1.04 us
    pallas_call x1, Pallas kernels, local(): pl.pallas_call(functools.partial(contract_kernel, beads_all), out_shape=[...  1.04 us
  transfers between devices with their start and end apart: 2, of which 2 were waited for; matrix products, arithmetic and copies ran while one was open for 0% of the time, Pallas kernels for 0%

profile of v5, /device:TPU:1, one launch (start us, length us, event | category | flops | bytes accessed | tf_op | source)
XLA Modules:
  0.0 40.4 jit_solution(2045790398961357643)
XLA Ops:
  0.0 1.0 %contract.1 = (f32[4,40,128]{2,1,0:T(8,128)S(1)}, f32[4,40,128]{2,1,0:T(8,128)S(1)}, f32[12,128]{1,0:T(8,128)S(1)}, f32[64,128]{1,0:T(8,128)S(1)}) custom-call(f32[3,8,1536]{2,1,0:T(8,128)} %bitcast.4, s32[3,128]{1,0:T(4,128)} %waves_from.1, s32[12,128]{1,0:T(8,128)} %bitcast.5, f32[1,4]{1,0:T(1,128)} %bitcast.6), custom_call_target="tpu_custom_call" | custom-call | tf_op jit(solution)/shard_map/contract/pallas_call | solution.py:414
  1.0 1.5 %collective-permute-start = (f32[4,40,128]{2,1,0:T(8,128)S(1)}, f32[4,40,128]{2,1,0:T(8,128)S(1)}, u32[]{:S(2)}, u32[]{:S(2)}) collective-permute-start(f32[4,40,128]{2,1,0:T(8,128)S(1)} %get-tuple-element.16), channel_id=1, source_target_pairs={{0,8},{8,0},{16,24},{24,16},{32,40},{40,32},{48,56},{56,48},{64,72... | collective-permute-start | bytes 245768 | tf_op jit(solution)/shard_map/ppermute | solution.py:395
  2.5 0.9 %collective-permute-done.taken_ref = f32[4,40,128]{2,1,0:T(8,128)S(1)} collective-permute-done((f32[4,40,128]{2,1,0:T(8,128)S(1)}, f32[4,40,128]{2,1,0:T(8,128)S(1)}, u32[]{:S(2)}, u32[]{:S(2)}) %collective-permute-start) | collective-permute-done | bytes 81952 | tf_op jit(solution)/shard_map/ppermute | solution.py:395
  3.5 11.4 %all_to_all.15.spots_ref = f32[8,48,128]{2,1,0:T(8,128)S(1)} all-to-all(f32[8,48,128]{2,1,0:T(8,128)S(1)} %pair_sum.1), channel_id=1, replica_groups={{80,64,112,96,16,0,48,32},{88,72,120,104,24,8,56,40},{81,65,113,97,17,1..., dimensions={0} | all-to-all | bytes 393216 | tf_op jit(solution)/shard_map/all_to_all | solution.py:390
  14.8 1.0 %structure.1 = (f32[8,24,256]{2,1,0:T(8,128)S(1)}, f32[32,128]{1,0:T(8,128)S(1)}, bf16[256,1536]{1,0:T(8,128)(2,1)S(1)}, bf16[256,1536]{1,0:T(8,128)(2,1)S(1)}, f32[32,1536]{1,0:T(8,128)S(1)}) custom-call(f32[8,48,128]{2,1,0:T(8,128)S(1)} %all_to_all.15.spots_ref, f32[12,128]{1,0:T(8,128)S(1)} %get-tuple-element.17.charge_ref), custom_call_target="tpu_custom_call" | custom-call | tf_op jit(solution)/shard_map/structure/pallas_call | solution.py:454
  15.9 9.7 %all_to_all.16.partial_ref = f32[8,24,256]{2,1,0:T(8,128)S(1)} all-to-all(f32[8,24,256]{2,1,0:T(8,128)S(1)} %get-tuple-element.18), channel_id=1, replica_groups={{5,4,7,6,1,0,3,2},{13,12,15,14,9,8,11,10},{21,20,23,22,17,16,19,18},{29..., dimensions={0} | all-to-all | bytes 393216 | tf_op jit(solution)/shard_map/all_to_all | solution.py:469
  25.6 0.5 %force.1 = f32[8,40,128]{2,1,0:T(8,128)S(1)} custom-call(f32[8,24,256]{2,1,0:T(8,128)S(1)} %all_to_all.16.partial_ref, f32[32,128]{1,0:T(8,128)S(1)} %get-tuple-element.19.weights_ref, bf16[256,1536]{1,0:T(8,128)(2,1)S(1)} %get-tuple-element.20.high_ref, bf16[256,1536]{1,0:T(8,128)(2,1)S(1)} %get-tuple-element.21.low_ref, ...), custom_call_target="tpu_custom_call" | custom-call | tf_op jit(solution)/shard_map/force/pallas_call | solution.py:472
  26.0 8.9 %all_to_all.17.force_ref = f32[8,40,128]{2,1,0:T(8,128)S(1)} all-to-all(f32[8,40,128]{2,1,0:T(8,128)S(1)} %force.1), channel_id=1, replica_groups={{80,64,112,96,16,0,48,32},{88,72,120,104,24,8,56,40},{81,65,113,97,17,1..., dimensions={0} | all-to-all | bytes 327680 | tf_op jit(solution)/shard_map/all_to_all | solution.py:390
  35.0 3.7 %collective-permute-start.1 = (f32[4,40,128]{2,1,0:T(8,128)S(1)}, f32[4,40,128]{2,1,0:T(8,128)S(1)}, u32[]{:S(2)}, u32[]{:S(2)}) collective-permute-start(f32[4,40,128]{2,1,0:T(8,128)S(1)} %gather.1.kept_ref), channel_id=1, source_target_pairs={{0,8},{8,0},{16,24},{24,16},{32,40},{40,32},{48,56},{56,48},{64,72... | collective-permute-start | bytes 245768 | tf_op jit(solution)/shard_map/ppermute | solution.py:395
  38.7 0.9 %collective-permute-done.1.taken_ref = f32[4,40,128]{2,1,0:T(8,128)S(1)} collective-permute-done((f32[4,40,128]{2,1,0:T(8,128)S(1)}, f32[4,40,128]{2,1,0:T(8,128)S(1)}, u32[]{:S(2)}, u32[]{:S(2)}) %collective-permute-start.1) | collective-permute-done | bytes 81952 | tf_op jit(solution)/shard_map/ppermute | solution.py:395
  39.6 0.8 %expand.1 = f32[3,8,1536]{2,1,0:T(8,128)} custom-call(f32[64,128]{1,0:T(8,128)S(1)} %get-tuple-element.14.table_ref, f32[4,40,128]{2,1,0:T(8,128)S(1)} %gather.1.kept_ref, f32[4,40,128]{2,1,0:T(8,128)S(1)} %collective-permute-done.1.taken_ref), custom_call_target="tpu_custom_call" | custom-call | tf_op jit(solution)/shard_map/expand/pallas_call | solution.py:492
  (2 shorter events, 0.0 us)
Async XLA Ops:
  1.0 2.4 %collective-permute-start = (f32[4,40,128]{2,1,0:T(8,128)S(1)}, f32[4,40,128]{2,1,0:T(8,128)S(1)}, u32[]{:S(2)}, u32[]{:S(2)}) collective-permute-start(f32[4,40,128]{2,1,0:T(8,128)S(1)} %get-tuple-element.16), channel_id=1, source_target_pairs={{0,8},{8,0},{16,24},{24,16},{32,40},{40,32},{48,56},{56,48},{64,72... | collective-permute-start | bytes 245768 | tf_op jit(solution)/shard_map/ppermute | solution.py:395
  35.0 4.6 %collective-permute-start.1 = (f32[4,40,128]{2,1,0:T(8,128)S(1)}, f32[4,40,128]{2,1,0:T(8,128)S(1)}, u32[]{:S(2)}, u32[]{:S(2)}) collective-permute-start(f32[4,40,128]{2,1,0:T(8,128)S(1)} %gather.1.kept_ref), channel_id=1, source_target_pairs={{0,8},{8,0},{16,24},{24,16},{32,40},{40,32},{48,56},{56,48},{64,72... | collective-permute-start | bytes 245768 | tf_op jit(solution)/shard_map/ppermute | solution.py:395

commit v6 on v5

--- a/solution.py
+++ b/solution.py
@@ -20,9 +20,9 @@
     nodes = 0.5 * np.cos(np.pi * (np.arange(400) + 0.5) / 400)
     u = nodes * nodes
     odd = np.linalg.lstsq(
-        nodes[:, None] * u[:, None] ** np.arange(7), np.sin(2 * np.pi * nodes), rcond=None
+        nodes[:, None] * u[:, None] ** np.arange(6), np.sin(2 * np.pi * nodes), rcond=None
     )[0]
-    even = np.linalg.lstsq(u[:, None] ** np.arange(8), np.cos(2 * np.pi * nodes), rcond=None)[0]
+    even = np.linalg.lstsq(u[:, None] ** np.arange(7), np.cos(2 * np.pi * nodes), rcond=None)[0]
     return [float(c) for c in odd], [float(c) for c in even]
 
 
@@ -211,19 +211,21 @@
     back = grid_row >= ROWS
     size = jnp.where(back, grid_row - ROWS, grid_row)
     wanted = jnp.where(back, jnp.where(size > 0, -size, 1000.0), size)
-    pair_row = iota((LANES, LANES), 0)
+    pair_row = iota((LANES, LANES), 0).astype(jnp.bfloat16)
+    wanted = wanted.astype(jnp.bfloat16)
+    one, zero = jnp.bfloat16(1.0), jnp.bfloat16(0.0)
     m1, m2, m3 = (
         jnp.concatenate([spots_ref[:, used + x, :], spots_ref[:, used + 3 + x, :]], axis=0)
         for x in range(3)
     )
     sign = jnp.where(m2 < 0, -1.0, 1.0)
     sign = jnp.where((m2 == 0) & (m3 < 0), -1.0, sign)
-    m1 = m1 * sign
-    place = place_of(m2 * sign, m3 * sign, half)
+    m1 = (m1 * sign).astype(jnp.bfloat16)
+    place = place_of(m2 * sign, m3 * sign, half).astype(jnp.bfloat16)
     counts = jnp.zeros((2 * ROWS, LANES), jnp.float32)
     for p in range(2 * peers):
-        left = jnp.where(wanted == m1[p : p + 1], 1.0, 0.0).astype(jnp.bfloat16)
-        right = jnp.where(pair_row == place[p : p + 1], 1.0, 0.0).astype(jnp.bfloat16)
+        left = jnp.where(wanted == m1[p : p + 1], one, zero)
+        right = jnp.where(pair_row == place[p : p + 1], one, zero)
         counts += dot_nt(left, right)
     m2, m3 = pair_of(iota((2 * ROWS, LANES), 1), half)
     square = size * size + m2 * m2 + m3 * m3

time: 40.6 us -> 40.6 us (level)
  no operation moved by 1% of the time
where the time goes in v6:
time: 40.6 us; the launch traced here: 40.3 us
  blocking collectives  30 us (74%)
  starting transfers between devices  5.14 us (13%)
  Pallas kernels  3.32 us (8%)
  waiting for transfers between devices  1.85 us (5%)
    all_to_all x2, blocking collectives, between_chips(): lax.all_to_all(array, 'bead', 0, 0, axis_index_groups=groups, tiled=True)  20.3 us
    all_to_all x1, blocking collectives, local(): lax.all_to_all(partial, 'atom', 0, 0, axis_index_groups=[members('factors...  9.7 us
    ppermute x2, starting transfers between devices, between_cores(): return lax.ppermute(array, 'bead', [(i, i ^ 1) for i in range(peers)])  5.14 us
    ppermute x2, waiting for transfers between devices, between_cores(): return lax.ppermute(array, 'bead', [(i, i ^ 1) for i in range(peers)])  1.85 us
    pallas_call x1, Pallas kernels, local(): pl.pallas_call(functools.partial(contract_kernel, beads_all), out_shape=[...  1.04 us
    pallas_call x1, Pallas kernels, local(): pl.pallas_call(functools.partial(structure_kernel, float(sites * atom_pee...  1.03 us
  transfers between devices with their start and end apart: 2, of which 2 were waited for; matrix products, arithmetic and copies ran while one was open for 0% of the time, Pallas kernels for 0%

profile of v6, /device:TPU:1, one launch (start us, length us, event | category | flops | bytes accessed | tf_op | source)
XLA Modules:
  0.0 40.3 jit_solution(9340282428760309129)
XLA Ops:
  0.0 1.0 %contract.1 = (f32[4,40,128]{2,1,0:T(8,128)S(1)}, f32[4,40,128]{2,1,0:T(8,128)S(1)}, f32[12,128]{1,0:T(8,128)S(1)}, f32[64,128]{1,0:T(8,128)S(1)}) custom-call(f32[3,8,1536]{2,1,0:T(8,128)} %bitcast.4, s32[3,128]{1,0:T(4,128)} %waves_from.1, s32[12,128]{1,0:T(8,128)} %bitcast.5, f32[1,4]{1,0:T(1,128)} %bitcast.6), custom_call_target="tpu_custom_call" | custom-call | tf_op jit(solution)/shard_map/contract/pallas_call | solution.py:416
  1.0 1.5 %collective-permute-start = (f32[4,40,128]{2,1,0:T(8,128)S(1)}, f32[4,40,128]{2,1,0:T(8,128)S(1)}, u32[]{:S(2)}, u32[]{:S(2)}) collective-permute-start(f32[4,40,128]{2,1,0:T(8,128)S(1)} %get-tuple-element.16), channel_id=1, source_target_pairs={{0,8},{8,0},{16,24},{24,16},{32,40},{40,32},{48,56},{56,48},{64,72... | collective-permute-start | bytes 245768 | tf_op jit(solution)/shard_map/ppermute | solution.py:397
  2.5 0.9 %collective-permute-done.taken_ref = f32[4,40,128]{2,1,0:T(8,128)S(1)} collective-permute-done((f32[4,40,128]{2,1,0:T(8,128)S(1)}, f32[4,40,128]{2,1,0:T(8,128)S(1)}, u32[]{:S(2)}, u32[]{:S(2)}) %collective-permute-start) | collective-permute-done | bytes 81952 | tf_op jit(solution)/shard_map/ppermute | solution.py:397
  3.5 11.4 %all_to_all.15.spots_ref = f32[8,48,128]{2,1,0:T(8,128)S(1)} all-to-all(f32[8,48,128]{2,1,0:T(8,128)S(1)} %pair_sum.1), channel_id=1, replica_groups={{80,64,112,96,16,0,48,32},{88,72,120,104,24,8,56,40},{81,65,113,97,17,1..., dimensions={0} | all-to-all | bytes 393216 | tf_op jit(solution)/shard_map/all_to_all | solution.py:392
  14.8 1.0 %structure.1 = (f32[8,24,256]{2,1,0:T(8,128)S(1)}, f32[32,128]{1,0:T(8,128)S(1)}, bf16[256,1536]{1,0:T(8,128)(2,1)S(1)}, bf16[256,1536]{1,0:T(8,128)(2,1)S(1)}, f32[32,1536]{1,0:T(8,128)S(1)}) custom-call(f32[8,48,128]{2,1,0:T(8,128)S(1)} %all_to_all.15.spots_ref, f32[12,128]{1,0:T(8,128)S(1)} %get-tuple-element.17.charge_ref), custom_call_target="tpu_custom_call" | custom-call | tf_op jit(solution)/shard_map/structure/pallas_call | solution.py:456
  15.9 9.7 %all_to_all.16.partial_ref = f32[8,24,256]{2,1,0:T(8,128)S(1)} all-to-all(f32[8,24,256]{2,1,0:T(8,128)S(1)} %get-tuple-element.18), channel_id=1, replica_groups={{5,4,7,6,1,0,3,2},{13,12,15,14,9,8,11,10},{21,20,23,22,17,16,19,18},{29..., dimensions={0} | all-to-all | bytes 393216 | tf_op jit(solution)/shard_map/all_to_all | solution.py:471
  25.6 0.5 %force.1 = f32[8,40,128]{2,1,0:T(8,128)S(1)} custom-call(f32[8,24,256]{2,1,0:T(8,128)S(1)} %all_to_all.16.partial_ref, f32[32,128]{1,0:T(8,128)S(1)} %get-tuple-element.19.weights_ref, bf16[256,1536]{1,0:T(8,128)(2,1)S(1)} %get-tuple-element.20.high_ref, bf16[256,1536]{1,0:T(8,128)(2,1)S(1)} %get-tuple-element.21.low_ref, ...), custom_call_target="tpu_custom_call" | custom-call | tf_op jit(solution)/shard_map/force/pallas_call | solution.py:474
  26.0 8.9 %all_to_all.17.force_ref = f32[8,40,128]{2,1,0:T(8,128)S(1)} all-to-all(f32[8,40,128]{2,1,0:T(8,128)S(1)} %force.1), channel_id=1, replica_groups={{80,64,112,96,16,0,48,32},{88,72,120,104,24,8,56,40},{81,65,113,97,17,1..., dimensions={0} | all-to-all | bytes 327680 | tf_op jit(solution)/shard_map/all_to_all | solution.py:392
  35.0 3.7 %collective-permute-start.1 = (f32[4,40,128]{2,1,0:T(8,128)S(1)}, f32[4,40,128]{2,1,0:T(8,128)S(1)}, u32[]{:S(2)}, u32[]{:S(2)}) collective-permute-start(f32[4,40,128]{2,1,0:T(8,128)S(1)} %gather.1.kept_ref), channel_id=1, source_target_pairs={{0,8},{8,0},{16,24},{24,16},{32,40},{40,32},{48,56},{56,48},{64,72... | collective-permute-start | bytes 245768 | tf_op jit(solution)/shard_map/ppermute | solution.py:397
  38.7 0.9 %collective-permute-done.1.taken_ref = f32[4,40,128]{2,1,0:T(8,128)S(1)} collective-permute-done((f32[4,40,128]{2,1,0:T(8,128)S(1)}, f32[4,40,128]{2,1,0:T(8,128)S(1)}, u32[]{:S(2)}, u32[]{:S(2)}) %collective-permute-start.1) | collective-permute-done | bytes 81952 | tf_op jit(solution)/shard_map/ppermute | solution.py:397
  39.6 0.8 %expand.1 = f32[3,8,1536]{2,1,0:T(8,128)} custom-call(f32[64,128]{1,0:T(8,128)S(1)} %get-tuple-element.14.table_ref, f32[4,40,128]{2,1,0:T(8,128)S(1)} %gather.1.kept_ref, f32[4,40,128]{2,1,0:T(8,128)S(1)} %collective-permute-done.1.taken_ref), custom_call_target="tpu_custom_call" | custom-call | tf_op jit(solution)/shard_map/expand/pallas_call | solution.py:494
  (2 shorter events, 0.0 us)
Async XLA Ops:
  1.0 2.4 %collective-permute-start = (f32[4,40,128]{2,1,0:T(8,128)S(1)}, f32[4,40,128]{2,1,0:T(8,128)S(1)}, u32[]{:S(2)}, u32[]{:S(2)}) collective-permute-start(f32[4,40,128]{2,1,0:T(8,128)S(1)} %get-tuple-element.16), channel_id=1, source_target_pairs={{0,8},{8,0},{16,24},{24,16},{32,40},{40,32},{48,56},{56,48},{64,72... | collective-permute-start | bytes 245768 | tf_op jit(solution)/shard_map/ppermute | solution.py:397
  35.0 4.6 %collective-permute-start.1 = (f32[4,40,128]{2,1,0:T(8,128)S(1)}, f32[4,40,128]{2,1,0:T(8,128)S(1)}, u32[]{:S(2)}, u32[]{:S(2)}) collective-permute-start(f32[4,40,128]{2,1,0:T(8,128)S(1)} %gather.1.kept_ref), channel_id=1, source_target_pairs={{0,8},{8,0},{16,24},{24,16},{32,40},{40,32},{48,56},{56,48},{64,72... | collective-permute-start | bytes 245768 | tf_op jit(solution)/shard_map/ppermute | solution.py:397

commit v7 on v6

--- a/solution.py
+++ b/solution.py
@@ -136,7 +136,8 @@
     tiles = points_ref.shape[2] // LANES
     bead_index = lax.axis_index("bead")
     first = (bead_index * beads).astype(jnp.float32)
-    start = (lax.rem(bead_index, 2) * (CONTR // 2)).astype(jnp.float32)
+    flip = flipped(lax.div(bead_index, 2))
+    start = (lax.rem(bead_index + flip, 2) * (CONTR // 2)).astype(jnp.float32)
     columns = [
         table_value(first + b, iota((CONTR, LANES), 0) + start, beads_all) for b in range(beads)
     ]
@@ -181,8 +182,12 @@
             out_ref[j * copies + c, used + 3 : used + 6, :] = taken_waves
 
 
+def members(key):
+    return [place ^ FIRST[key] for place in range(8)]
+
+
 def own_half():
-    first = ORDERS["spots"]
+    first = FIRST["spots"]
     bit = lax.rem(lax.div(lax.axis_index("bead"), 2) + first % 2, 2)
     return bit.astype(jnp.float32)
 
@@ -380,16 +385,29 @@
 PARAMS = pltpu.CompilerParams(vmem_limit_bytes=24 * 1024 * 1024)
 
 
-ORDERS = {"spots": 5, "factors": 5, "forces": 5}
-
-
-def members(key):
-    return [place ^ ORDERS[key] for place in range(8)]
-
-
-def between_chips(array, key):
-    groups = [[2 * chip + core for chip in members(key)] for core in range(2)]
-    return lax.all_to_all(array, "bead", 0, 0, axis_index_groups=groups, tiled=True)
+FIRST = {"spots": 5, "factors": 5, "forces": 5}
+
+
+def flipped(chip):
+    return lax.div(chip, 4) if isinstance(chip, jax.Array) else chip // 4
+
+
+def between(array, key):
+    count = 8
+    groups = []
+    for side in range(2):
+        for index in range(count):
+            group = []
+            for place in range(count):
+                chip, block = place ^ FIRST[key], index
+                if key == "factors":
+                    chip, block = block, chip
+                core = side ^ flipped(chip)
+                group.append((2 * chip + core) * count + block)
+            groups.append(group)
+    return lax.all_to_all(
+        array, ("bead", "atom"), 0, 0, axis_index_groups=groups, tiled=True
+    )
 
 
 def between_cores(array):
@@ -424,7 +442,7 @@
         in_specs=[HBM] * 4,
         out_specs=[VMEM] * 4,
         scratch_shapes=[
-            pltpu.VMEM((used * CONTR, LANES), jnp.float32),
+            pltpu.VMEM((rows * CONTR, LANES), jnp.float32),
             pltpu.VMEM((3, beads, sites), jnp.float32),
             pltpu.VMEM(waves.shape, jnp.int32),
             pltpu.VMEM((tiles, LANES), jnp.int32),
@@ -452,7 +470,7 @@
         compiler_params=PARAMS,
         name="pair_sum",
     )(kept, between_cores(given))
-    spots = between_chips(portion, "spots")
+    spots = between(portion, "spots")
     partial, weights, high, low, plain = pl.pallas_call(
         functools.partial(structure_kernel, float(sites * atom_peers)),
         out_shape=[
@@ -468,9 +486,7 @@
         compiler_params=PARAMS,
         name="structure",
     )(spots, charge)
-    factors = lax.all_to_all(
-        partial, "atom", 0, 0, axis_index_groups=[members("factors")], tiled=True
-    )
+    factors = between(partial, "factors")
     force = pl.pallas_call(
         force_kernel,
         out_shape=shaped(chips, held, LANES),
@@ -490,7 +506,7 @@
         out_specs=VMEM,
         compiler_params=PARAMS,
         name="gather",
-    )(between_chips(force, "forces"))
+    )(between(force, "forces"))
     out = pl.pallas_call(
         expand_kernel,
         out_shape=shaped(3, beads, sites),

time: 40.6 us -> 40.2 us (level)
  starting transfers between devices: 5.14 us -> 1.94 us
  blocking collectives: 30 us -> 32.8 us
    ppermute x2, starting transfers between devices: 5.14 us -> 1.94 us  [between_cores(): return lax.ppermute(array, 'bead', [(i, i ^ 1) for i in range(peers)])]
    all_to_all x3, blocking collectives: 30 us -> 32.8 us  [between(): lax.all_to_all(array, ('bead', 'atom'), 0, 0, axis_index_groups=groups, t...]
where the time goes in v7:
time: 40.2 us; the launch traced here: 40 us
  blocking collectives  32.8 us (82%)
  Pallas kernels  3.32 us (8%)
  starting transfers between devices  1.94 us (5%)
  waiting for transfers between devices  1.85 us (5%)
    all_to_all x3, blocking collectives, between(): lax.all_to_all(array, ('bead', 'atom'), 0, 0, axis_index_groups=groups, t...  32.8 us
    ppermute x2, starting transfers between devices, between_cores(): return lax.ppermute(array, 'bead', [(i, i ^ 1) for i in range(peers)])  1.94 us
    ppermute x2, waiting for transfers between devices, between_cores(): return lax.ppermute(array, 'bead', [(i, i ^ 1) for i in range(peers)])  1.85 us
    pallas_call x1, Pallas kernels, local(): pl.pallas_call(functools.partial(contract_kernel, beads_all), out_shape=[...  1.04 us
    pallas_call x1, Pallas kernels, local(): pl.pallas_call(functools.partial(structure_kernel, float(sites * atom_pee...  1.03 us
  transfers between devices with their start and end apart: 2, of which 2 were waited for; matrix products, arithmetic and copies ran while one was open for 0% of the time, Pallas kernels for 0%

profile of v7, /device:TPU:1, one launch (start us, length us, event | category | flops | bytes accessed | tf_op | source)
XLA Modules:
  0.0 40.0 jit_solution(14511698297205052431)
XLA Ops:
  0.0 1.0 %contract.1 = (f32[4,40,128]{2,1,0:T(8,128)S(1)}, f32[4,40,128]{2,1,0:T(8,128)S(1)}, f32[12,128]{1,0:T(8,128)S(1)}, f32[64,128]{1,0:T(8,128)S(1)}) custom-call(f32[3,8,1536]{2,1,0:T(8,128)} %bitcast.4, s32[3,128]{1,0:T(4,128)} %waves_from.1, s32[12,128]{1,0:T(8,128)} %bitcast.5, f32[1,4]{1,0:T(1,128)} %bitcast.6), custom_call_target="tpu_custom_call" | custom-call | tf_op jit(solution)/shard_map/contract/pallas_call | solution.py:434
  1.0 1.5 %collective-permute-start = (f32[4,40,128]{2,1,0:T(8,128)S(1)}, f32[4,40,128]{2,1,0:T(8,128)S(1)}, u32[]{:S(2)}, u32[]{:S(2)}) collective-permute-start(f32[4,40,128]{2,1,0:T(8,128)S(1)} %get-tuple-element.16), channel_id=1, source_target_pairs={{0,8},{8,0},{16,24},{24,16},{32,40},{40,32},{48,56},{56,48},{64,72... | collective-permute-start | bytes 245768 | tf_op jit(solution)/shard_map/ppermute | solution.py:415
  2.5 0.9 %collective-permute-done.taken_ref = f32[4,40,128]{2,1,0:T(8,128)S(1)} collective-permute-done((f32[4,40,128]{2,1,0:T(8,128)S(1)}, f32[4,40,128]{2,1,0:T(8,128)S(1)}, u32[]{:S(2)}, u32[]{:S(2)}) %collective-permute-start) | collective-permute-done | bytes 81952 | tf_op jit(solution)/shard_map/ppermute | solution.py:415
  3.5 11.4 %all_to_all.15.spots_ref = f32[8,48,128]{2,1,0:T(8,128)S(1)} all-to-all(f32[8,48,128]{2,1,0:T(8,128)S(1)} %pair_sum.1), channel_id=1, replica_groups={{88,72,120,104,16,0,48,32},{89,73,121,105,17,1,49,33},{90,74,122,106,18..., dimensions={0} | all-to-all | bytes 393216 | tf_op jit(solution)/shard_map/all_to_all | solution.py:408
  14.9 1.0 %structure.1 = (f32[8,24,256]{2,1,0:T(8,128)S(1)}, f32[32,128]{1,0:T(8,128)S(1)}, bf16[256,1536]{1,0:T(8,128)(2,1)S(1)}, bf16[256,1536]{1,0:T(8,128)(2,1)S(1)}, f32[32,1536]{1,0:T(8,128)S(1)}) custom-call(f32[8,48,128]{2,1,0:T(8,128)S(1)} %all_to_all.15.spots_ref, f32[12,128]{1,0:T(8,128)S(1)} %get-tuple-element.17.charge_ref), custom_call_target="tpu_custom_call" | custom-call | tf_op jit(solution)/shard_map/structure/pallas_call | solution.py:474
  15.9 9.7 %all_to_all.16.partial_ref = f32[8,24,256]{2,1,0:T(8,128)S(1)} all-to-all(f32[8,24,256]{2,1,0:T(8,128)S(1)} %get-tuple-element.18), channel_id=1, replica_groups={{5,4,7,6,1,0,3,2},{21,20,23,22,17,16,19,18},{37,36,39,38,33,32,35,34},{..., dimensions={0} | all-to-all | bytes 393216 | tf_op jit(solution)/shard_map/all_to_all | solution.py:408
  25.6 0.5 %force.1 = f32[8,40,128]{2,1,0:T(8,128)S(1)} custom-call(f32[8,24,256]{2,1,0:T(8,128)S(1)} %all_to_all.16.partial_ref, f32[32,128]{1,0:T(8,128)S(1)} %get-tuple-element.19.weights_ref, bf16[256,1536]{1,0:T(8,128)(2,1)S(1)} %get-tuple-element.20.high_ref, bf16[256,1536]{1,0:T(8,128)(2,1)S(1)} %get-tuple-element.21.low_ref, ...), custom_call_target="tpu_custom_call" | custom-call | tf_op jit(solution)/shard_map/force/pallas_call | solution.py:490
  26.1 11.7 %all_to_all.17.force_ref = f32[8,40,128]{2,1,0:T(8,128)S(1)} all-to-all(f32[8,40,128]{2,1,0:T(8,128)S(1)} %force.1), channel_id=1, replica_groups={{88,72,120,104,16,0,48,32},{89,73,121,105,17,1,49,33},{90,74,122,106,18..., dimensions={0} | all-to-all | bytes 327680 | tf_op jit(solution)/shard_map/all_to_all | solution.py:408
  37.8 0.5 %collective-permute-start.1 = (f32[4,40,128]{2,1,0:T(8,128)S(1)}, f32[4,40,128]{2,1,0:T(8,128)S(1)}, u32[]{:S(2)}, u32[]{:S(2)}) collective-permute-start(f32[4,40,128]{2,1,0:T(8,128)S(1)} %gather.1.kept_ref), channel_id=1, source_target_pairs={{0,8},{8,0},{16,24},{24,16},{32,40},{40,32},{48,56},{56,48},{64,72... | collective-permute-start | bytes 245768 | tf_op jit(solution)/shard_map/ppermute | solution.py:415
  38.3 0.9 %collective-permute-done.1.taken_ref = f32[4,40,128]{2,1,0:T(8,128)S(1)} collective-permute-done((f32[4,40,128]{2,1,0:T(8,128)S(1)}, f32[4,40,128]{2,1,0:T(8,128)S(1)}, u32[]{:S(2)}, u32[]{:S(2)}) %collective-permute-start.1) | collective-permute-done | bytes 81952 | tf_op jit(solution)/shard_map/ppermute | solution.py:415
  39.2 0.8 %expand.1 = f32[3,8,1536]{2,1,0:T(8,128)} custom-call(f32[64,128]{1,0:T(8,128)S(1)} %get-tuple-element.14.table_ref, f32[4,40,128]{2,1,0:T(8,128)S(1)} %gather.1.kept_ref, f32[4,40,128]{2,1,0:T(8,128)S(1)} %collective-permute-done.1.taken_ref), custom_call_target="tpu_custom_call" | custom-call | tf_op jit(solution)/shard_map/expand/pallas_call | solution.py:510
  (2 shorter events, 0.0 us)
Async XLA Ops:
  1.0 2.4 %collective-permute-start = (f32[4,40,128]{2,1,0:T(8,128)S(1)}, f32[4,40,128]{2,1,0:T(8,128)S(1)}, u32[]{:S(2)}, u32[]{:S(2)}) collective-permute-start(f32[4,40,128]{2,1,0:T(8,128)S(1)} %get-tuple-element.16), channel_id=1, source_target_pairs={{0,8},{8,0},{16,24},{24,16},{32,40},{40,32},{48,56},{56,48},{64,72... | collective-permute-start | bytes 245768 | tf_op jit(solution)/shard_map/ppermute | solution.py:415
  37.8 1.4 %collective-permute-start.1 = (f32[4,40,128]{2,1,0:T(8,128)S(1)}, f32[4,40,128]{2,1,0:T(8,128)S(1)}, u32[]{:S(2)}, u32[]{:S(2)}) collective-permute-start(f32[4,40,128]{2,1,0:T(8,128)S(1)} %gather.1.kept_ref), channel_id=1, source_target_pairs={{0,8},{8,0},{16,24},{24,16},{32,40},{40,32},{48,56},{56,48},{64,72... | collective-permute-start | bytes 245768 | tf_op jit(solution)/shard_map/ppermute | solution.py:415

commit v8 on v7

--- a/solution.py
+++ b/solution.py
@@ -112,11 +112,10 @@
     waves_from,
     labels_from,
     species_from,
-    kept_ref,
+    work_ref,
     given_ref,
     charge_ref,
     table_ref,
-    work_ref,
     points_ref,
     waves_ref,
     labels_ref,
@@ -154,14 +153,12 @@
             work_ref[row : row + CONTR, :] = total
     used = 3 * tiles
     half = CONTR // 2
-    for target, begin in ((given_ref, half), (kept_ref, 0)):
-        for j in range(half):
-            target[j, 0:used, :] = work_ref[pl.ds(begin + j, used, stride=CONTR), :]
+    for j in range(half):
+        given_ref[j, 0:used, :] = work_ref[pl.ds(half + j, used, stride=CONTR), :]
     for copy in copies_in[3:]:
         copy.wait()
     waves = waves_ref[...].astype(jnp.float32)
-    for target in (given_ref, kept_ref):
-        target[0, used : used + 3, :] = waves
+    given_ref[0, used : used + 3, :] = waves
     labels = labels_ref[...]
     charge = jnp.zeros(labels.shape, jnp.float32)
     for kind in range(species_ref.shape[1]):
@@ -170,12 +167,12 @@
     charge_ref[...] = charge
 
 
-def pair_sum_kernel(used, kept_ref, taken_ref, out_ref):
-    copies = out_ref.shape[0] // kept_ref.shape[0]
-    kept_waves = kept_ref[0, used : used + 3, :]
+def pair_sum_kernel(used, work_ref, given_ref, taken_ref, out_ref):
+    copies = out_ref.shape[0] // given_ref.shape[0]
+    kept_waves = given_ref[0, used : used + 3, :]
     taken_waves = taken_ref[0, used : used + 3, :]
-    for j in range(kept_ref.shape[0]):
-        total = kept_ref[j, 0:used, :] + taken_ref[j, 0:used, :]
+    for j in range(given_ref.shape[0]):
+        total = work_ref[pl.ds(j, used, stride=CONTR), :] + taken_ref[j, 0:used, :]
         for c in range(copies):
             out_ref[j * copies + c, 0:used, :] = total
             out_ref[j * copies + c, used : used + 3, :] = kept_waves
@@ -348,7 +345,17 @@
         out_ref[j, 0:used, :] = total
 
 
-def expand_kernel(table_ref, kept_ref, taken_ref, out_to, work_ref, out_ref, sems):
+def own_kernel(used, table_ref, kept_ref, out_ref):
+    parts = [kept_ref[j, 0:used, :] for j in range(kept_ref.shape[0])]
+    for b in range(out_ref.shape[0]):
+        at = b * CONTR
+        total = parts[0] * table_ref[at : at + 1]
+        for j in range(1, len(parts)):
+            total += parts[j] * table_ref[at + j : at + j + 1]
+        out_ref[b, 0:used, :] = total
+
+
+def expand_kernel(table_ref, own_ref, taken_ref, out_to, work_ref, out_ref, sems):
     beads = out_ref.shape[1]
     tiles = out_ref.shape[2] // LANES
     used = 3 * tiles
@@ -358,13 +365,11 @@
     moves = []
     for r in range(0, used, 8):
         size = min(8, used - r)
-        parts = [
-            source[j, r : r + size, :] for source in (kept_ref, taken_ref) for j in range(CONTR // 2)
-        ]
+        parts = [taken_ref[j, r : r + size, :] for j in range(CONTR // 2)]
         for b in range(beads):
-            at = b * CONTR
-            total = parts[0] * table[at : at + 1]
-            for j in range(1, CONTR):
+            at = b * CONTR + CONTR // 2
+            total = own_ref[b, r : r + size, :]
+            for j in range(CONTR // 2):
                 total += parts[j] * table[at + j : at + j + 1]
             work_ref[b * stride + r : b * stride + r + size, :] = total
         for i in range(r, r + size):
@@ -431,10 +436,10 @@
     half = CONTR // 2
     chips = bead_peers // 2
     beads_all = beads * bead_peers
-    kept, given, charge, table = pl.pallas_call(
+    work, given, charge, table = pl.pallas_call(
         functools.partial(contract_kernel, beads_all),
         out_shape=[
-            shaped(half, rows, LANES),
+            shaped(rows * CONTR, LANES),
             shaped(half, rows, LANES),
             shaped(tiles, LANES),
             shaped(beads * CONTR, LANES),
@@ -442,7 +447,6 @@
         in_specs=[HBM] * 4,
         out_specs=[VMEM] * 4,
         scratch_shapes=[
-            pltpu.VMEM((rows * CONTR, LANES), jnp.float32),
             pltpu.VMEM((3, beads, sites), jnp.float32),
             pltpu.VMEM(waves.shape, jnp.int32),
             pltpu.VMEM((tiles, LANES), jnp.int32),
@@ -465,11 +469,11 @@
     portion = pl.pallas_call(
         functools.partial(pair_sum_kernel, used),
         out_shape=shaped(chips, sent, LANES),
-        in_specs=[VMEM] * 2,
+        in_specs=[VMEM] * 3,
         out_specs=VMEM,
         compiler_params=PARAMS,
         name="pair_sum",
-    )(kept, between_cores(given))
+    )(work, given, between_cores(given))
     spots = between(portion, "spots")
     partial, weights, high, low, plain = pl.pallas_call(
         functools.partial(structure_kernel, float(sites * atom_peers)),
@@ -507,6 +511,16 @@
         compiler_params=PARAMS,
         name="gather",
     )(between(force, "forces"))
+    taken = between_cores(gathered)
+    own = pl.pallas_call(
+        functools.partial(own_kernel, used),
+        out_shape=shaped(beads, held, LANES),
+        in_specs=[VMEM] * 2,
+        out_specs=VMEM,
+        compiler_params=PARAMS,
+        cost_estimate=pl.CostEstimate(flops=300000, bytes_accessed=300000, transcendentals=0),
+        name="own",
+    )(table, gathered)
     out = pl.pallas_call(
         expand_kernel,
         out_shape=shaped(3, beads, sites),
@@ -519,7 +533,7 @@
         ],
         compiler_params=PARAMS,
         name="expand",
-    )(table, gathered, between_cores(gathered))
+    )(table, own, taken)
     return out.transpose(1, 0, 2)
 
 

time: 40.2 us -> 40.2 us (level)
  no operation moved by 1% of the time
where the time goes in v8:
time: 40.2 us; the launch traced here: 39.9 us
  blocking collectives  32.8 us (82%)
  Pallas kernels  3.32 us (8%)
  starting transfers between devices  1.93 us (5%)
  waiting for transfers between devices  1.8 us (4%)
    all_to_all x3, blocking collectives, between(): lax.all_to_all(array, ('bead', 'atom'), 0, 0, axis_index_groups=groups, t...  32.8 us
    ppermute x2, starting transfers between devices, between_cores(): return lax.ppermute(array, 'bead', [(i, i ^ 1) for i in range(peers)])  1.93 us
    ppermute x2, waiting for transfers between devices, between_cores(): return lax.ppermute(array, 'bead', [(i, i ^ 1) for i in range(peers)])  1.8 us
    pallas_call x1, Pallas kernels, local(): pl.pallas_call(functools.partial(contract_kernel, beads_all), out_shape=[...  1.03 us
    pallas_call x1, Pallas kernels, local(): pl.pallas_call(functools.partial(structure_kernel, float(sites * atom_pee...  1.02 us
  transfers between devices with their start and end apart: 2, of which 2 were waited for; matrix products, arithmetic and copies ran while one was open for 0% of the time, Pallas kernels for 0%

profile of v8, /device:TPU:1, one launch (start us, length us, event | category | flops | bytes accessed | tf_op | source)
XLA Modules:
  0.0 39.9 jit_solution(9798090638977022827)
XLA Ops:
  0.0 1.0 %contract.1 = (f32[320,128]{1,0:T(8,128)S(1)}, f32[4,40,128]{2,1,0:T(8,128)S(1)}, f32[12,128]{1,0:T(8,128)S(1)}, f32[64,128]{1,0:T(8,128)S(1)}) custom-call(f32[3,8,1536]{2,1,0:T(8,128)} %bitcast.4, s32[3,128]{1,0:T(4,128)} %waves_from.1, s32[12,128]{1,0:T(8,128)} %bitcast.5, f32[1,4]{1,0:T(1,128)} %bitcast.6), custom_call_target="tpu_custom_call" | custom-call | tf_op jit(solution)/shard_map/contract/pallas_call | solution.py:439
  1.0 1.5 %collective-permute-start = (f32[4,40,128]{2,1,0:T(8,128)S(1)}, f32[4,40,128]{2,1,0:T(8,128)S(1)}, u32[]{:S(2)}, u32[]{:S(2)}) collective-permute-start(f32[4,40,128]{2,1,0:T(8,128)S(1)} %get-tuple-element.16.given_ref), channel_id=1, source_target_pairs={{0,8},{8,0},{16,24},{24,16},{32,40},{40,32},{48,56},{56,48},{64,72... | collective-permute-start | bytes 245768 | tf_op jit(solution)/shard_map/ppermute | solution.py:420
  2.5 0.9 %collective-permute-done.taken_ref = f32[4,40,128]{2,1,0:T(8,128)S(1)} collective-permute-done((f32[4,40,128]{2,1,0:T(8,128)S(1)}, f32[4,40,128]{2,1,0:T(8,128)S(1)}, u32[]{:S(2)}, u32[]{:S(2)}) %collective-permute-start) | collective-permute-done | bytes 81952 | tf_op jit(solution)/shard_map/ppermute | solution.py:420
  3.5 11.4 %all_to_all.15.spots_ref = f32[8,48,128]{2,1,0:T(8,128)S(1)} all-to-all(f32[8,48,128]{2,1,0:T(8,128)S(1)} %pair_sum.1), channel_id=1, replica_groups={{88,72,120,104,16,0,48,32},{89,73,121,105,17,1,49,33},{90,74,122,106,18..., dimensions={0} | all-to-all | bytes 393216 | tf_op jit(solution)/shard_map/all_to_all | solution.py:413
  14.9 1.0 %structure.1 = (f32[8,24,256]{2,1,0:T(8,128)S(1)}, f32[32,128]{1,0:T(8,128)S(1)}, bf16[256,1536]{1,0:T(8,128)(2,1)S(1)}, bf16[256,1536]{1,0:T(8,128)(2,1)S(1)}, f32[32,1536]{1,0:T(8,128)S(1)}) custom-call(f32[8,48,128]{2,1,0:T(8,128)S(1)} %all_to_all.15.spots_ref, f32[12,128]{1,0:T(8,128)S(1)} %get-tuple-element.17.charge_ref), custom_call_target="tpu_custom_call" | custom-call | tf_op jit(solution)/shard_map/structure/pallas_call | solution.py:478
  15.9 9.7 %all_to_all.16.partial_ref = f32[8,24,256]{2,1,0:T(8,128)S(1)} all-to-all(f32[8,24,256]{2,1,0:T(8,128)S(1)} %get-tuple-element.18), channel_id=1, replica_groups={{5,4,7,6,1,0,3,2},{21,20,23,22,17,16,19,18},{37,36,39,38,33,32,35,34},{..., dimensions={0} | all-to-all | bytes 393216 | tf_op jit(solution)/shard_map/all_to_all | solution.py:413
  25.6 0.5 %force.1 = f32[8,40,128]{2,1,0:T(8,128)S(1)} custom-call(f32[8,24,256]{2,1,0:T(8,128)S(1)} %all_to_all.16.partial_ref, f32[32,128]{1,0:T(8,128)S(1)} %get-tuple-element.19.weights_ref, bf16[256,1536]{1,0:T(8,128)(2,1)S(1)} %get-tuple-element.20.high_ref, bf16[256,1536]{1,0:T(8,128)(2,1)S(1)} %get-tuple-element.21.low_ref, ...), custom_call_target="tpu_custom_call" | custom-call | tf_op jit(solution)/shard_map/force/pallas_call | solution.py:494
  26.1 11.7 %all_to_all.17.force_ref = f32[8,40,128]{2,1,0:T(8,128)S(1)} all-to-all(f32[8,40,128]{2,1,0:T(8,128)S(1)} %force.1), channel_id=1, replica_groups={{88,72,120,104,16,0,48,32},{89,73,121,105,17,1,49,33},{90,74,122,106,18..., dimensions={0} | all-to-all | bytes 327680 | tf_op jit(solution)/shard_map/all_to_all | solution.py:413
  37.8 0.5 %collective-permute-start.1 = (f32[4,40,128]{2,1,0:T(8,128)S(1)}, f32[4,40,128]{2,1,0:T(8,128)S(1)}, u32[]{:S(2)}, u32[]{:S(2)}) collective-permute-start(f32[4,40,128]{2,1,0:T(8,128)S(1)} %gather.1.kept_ref), channel_id=1, source_target_pairs={{0,8},{8,0},{16,24},{24,16},{32,40},{40,32},{48,56},{56,48},{64,72... | collective-permute-start | bytes 245768 | tf_op jit(solution)/shard_map/ppermute | solution.py:420
  38.3 0.9 %collective-permute-done.1.taken_ref = f32[4,40,128]{2,1,0:T(8,128)S(1)} collective-permute-done((f32[4,40,128]{2,1,0:T(8,128)S(1)}, f32[4,40,128]{2,1,0:T(8,128)S(1)}, u32[]{:S(2)}, u32[]{:S(2)}) %collective-permute-start.1) | collective-permute-done | bytes 81952 | tf_op jit(solution)/shard_map/ppermute | solution.py:420
  39.2 0.7 %expand.1 = f32[3,8,1536]{2,1,0:T(8,128)} custom-call(f32[64,128]{1,0:T(8,128)S(1)} %get-tuple-element.14.table_ref, f32[8,40,128]{2,1,0:T(8,128)S(1)} %own.1.own_ref, f32[4,40,128]{2,1,0:T(8,128)S(1)} %collective-permute-done.1.taken_ref), custom_call_target="tpu_custom_call" | custom-call | tf_op jit(solution)/shard_map/expand/pallas_call | solution.py:524
  (3 shorter events, 0.1 us)
Async XLA Ops:
  1.0 2.4 %collective-permute-start = (f32[4,40,128]{2,1,0:T(8,128)S(1)}, f32[4,40,128]{2,1,0:T(8,128)S(1)}, u32[]{:S(2)}, u32[]{:S(2)}) collective-permute-start(f32[4,40,128]{2,1,0:T(8,128)S(1)} %get-tuple-element.16.given_ref), channel_id=1, source_target_pairs={{0,8},{8,0},{16,24},{24,16},{32,40},{40,32},{48,56},{56,48},{64,72... | collective-permute-start | bytes 245768 | tf_op jit(solution)/shard_map/ppermute | solution.py:420
  37.8 1.4 %collective-permute-start.1 = (f32[4,40,128]{2,1,0:T(8,128)S(1)}, f32[4,40,128]{2,1,0:T(8,128)S(1)}, u32[]{:S(2)}, u32[]{:S(2)}) collective-permute-start(f32[4,40,128]{2,1,0:T(8,128)S(1)} %gather.1.kept_ref), channel_id=1, source_target_pairs={{0,8},{8,0},{16,24},{24,16},{32,40},{40,32},{48,56},{56,48},{64,72... | collective-permute-start | bytes 245768 | tf_op jit(solution)/shard_map/ppermute | solution.py:420

commit v9 on v8

--- a/solution.py
+++ b/solution.py
@@ -246,7 +246,7 @@
         for index, value in enumerate(both_turns(size * x1)):
             value = q * value
             at = index * ROWS
-            plain_ref[at : at + ROWS, lanes] = value
+            plain_ref[index * SENT : (index + 1) * SENT, lanes] = value[0:SENT]
             high, low = split(value)
             charged_ref[at : at + ROWS, lanes] = high
             charged_ref[2 * ROWS + at : 3 * ROWS + at, lanes] = low
@@ -304,12 +304,12 @@
     )
     m1 = TWO_PI * iota((SENT, LANES), 0)
     for kind, (on_cos, on_sin) in enumerate(rows):
-        at = (1 - kind) * ROWS
+        at = (1 - kind) * SENT
         along = m1 if kind == 0 else -m1
         coef_ref[at : at + SENT, :LANES] = along * on_cos
         coef_ref[at : at + SENT, LANES:] = along * on_sin
         for axis, m in enumerate((m2, m3)):
-            at = kind * ROWS + 2 * ROWS * (axis + 1)
+            at = kind * SENT + 2 * SENT * (axis + 1)
             coef_ref[at : at + SENT, :LANES] = (-TWO_PI) * m * on_sin
             coef_ref[at : at + SENT, LANES:] = TWO_PI * m * on_cos
     high, low = split(coef_ref[...])
@@ -323,8 +323,8 @@
         term = near[:size] + near[size:] + far
         plain = plain_ref[:, lanes]
         for x in range(3):
-            at = 2 * ROWS * x
-            total = jnp.sum(term[at : at + 2 * ROWS] * plain, axis=0, keepdims=True)
+            at = 2 * SENT * x
+            total = jnp.sum(term[at : at + 2 * SENT] * plain, axis=0, keepdims=True)
             for i in range(2):
                 term_ref[x * tiles + t + i : x * tiles + t + i + 1, :] = total[
                     :, i * LANES : (i + 1) * LANES
@@ -482,7 +482,7 @@
             shaped(2 * ROWS, LANES),
             shaped(2 * LANES, sites, dtype=jnp.bfloat16),
             shaped(2 * LANES, sites, dtype=jnp.bfloat16),
-            shaped(2 * ROWS, sites),
+            shaped(2 * SENT, sites),
         ],
         in_specs=[VMEM] * 2,
         out_specs=[VMEM] * 5,
@@ -497,7 +497,7 @@
         in_specs=[VMEM] * 5,
         out_specs=VMEM,
         scratch_shapes=[
-            pltpu.VMEM((6 * ROWS, 2 * LANES), jnp.float32),
+            pltpu.VMEM((-(-6 * SENT // 16) * 16, 2 * LANES), jnp.float32),
             pltpu.VMEM((used, LANES), jnp.float32),
         ],
         compiler_params=PARAMS,

time: 40.2 us -> 40.2 us (level)
  no operation moved by 1% of the time
where the time goes in v9:
time: 40.2 us; the launch traced here: 39.9 us
  blocking collectives  32.9 us (82%)
  Pallas kernels  3.3 us (8%)
  starting transfers between devices  1.94 us (5%)
  waiting for transfers between devices  1.8 us (4%)
    all_to_all x3, blocking collectives, between(): lax.all_to_all(array, ('bead', 'atom'), 0, 0, axis_index_groups=groups, t...  32.9 us
    ppermute x2, starting transfers between devices, between_cores(): return lax.ppermute(array, 'bead', [(i, i ^ 1) for i in range(peers)])  1.94 us
    ppermute x2, waiting for transfers between devices, between_cores(): return lax.ppermute(array, 'bead', [(i, i ^ 1) for i in range(peers)])  1.8 us
    pallas_call x1, Pallas kernels, local(): pl.pallas_call(functools.partial(contract_kernel, beads_all), out_shape=[...  1.03 us
    pallas_call x1, Pallas kernels, local(): pl.pallas_call(functools.partial(structure_kernel, float(sites * atom_pee...  1.02 us
  transfers between devices with their start and end apart: 2, of which 2 were waited for; matrix products, arithmetic and copies ran while one was open for 0% of the time, Pallas kernels for 0%

profile of v9, /device:TPU:1, one launch (start us, length us, event | category | flops | bytes accessed | tf_op | source)
XLA Modules:
  0.0 39.9 jit_solution(15801633412284446969)
XLA Ops:
  0.0 1.0 %contract.1 = (f32[320,128]{1,0:T(8,128)S(1)}, f32[4,40,128]{2,1,0:T(8,128)S(1)}, f32[12,128]{1,0:T(8,128)S(1)}, f32[64,128]{1,0:T(8,128)S(1)}) custom-call(f32[3,8,1536]{2,1,0:T(8,128)} %bitcast.4, s32[3,128]{1,0:T(4,128)} %waves_from.1, s32[12,128]{1,0:T(8,128)} %bitcast.5, f32[1,4]{1,0:T(1,128)} %bitcast.6), custom_call_target="tpu_custom_call" | custom-call | tf_op jit(solution)/shard_map/contract/pallas_call | solution.py:439
  1.0 1.5 %collective-permute-start = (f32[4,40,128]{2,1,0:T(8,128)S(1)}, f32[4,40,128]{2,1,0:T(8,128)S(1)}, u32[]{:S(2)}, u32[]{:S(2)}) collective-permute-start(f32[4,40,128]{2,1,0:T(8,128)S(1)} %get-tuple-element.16.given_ref), channel_id=1, source_target_pairs={{0,8},{8,0},{16,24},{24,16},{32,40},{40,32},{48,56},{56,48},{64,72... | collective-permute-start | bytes 245768 | tf_op jit(solution)/shard_map/ppermute | solution.py:420
  2.5 0.9 %collective-permute-done.taken_ref = f32[4,40,128]{2,1,0:T(8,128)S(1)} collective-permute-done((f32[4,40,128]{2,1,0:T(8,128)S(1)}, f32[4,40,128]{2,1,0:T(8,128)S(1)}, u32[]{:S(2)}, u32[]{:S(2)}) %collective-permute-start) | collective-permute-done | bytes 81952 | tf_op jit(solution)/shard_map/ppermute | solution.py:420
  3.5 11.4 %all_to_all.15.spots_ref = f32[8,48,128]{2,1,0:T(8,128)S(1)} all-to-all(f32[8,48,128]{2,1,0:T(8,128)S(1)} %pair_sum.1), channel_id=1, replica_groups={{88,72,120,104,16,0,48,32},{89,73,121,105,17,1,49,33},{90,74,122,106,18..., dimensions={0} | all-to-all | bytes 393216 | tf_op jit(solution)/shard_map/all_to_all | solution.py:413
  14.9 1.0 %structure.1 = (f32[8,24,256]{2,1,0:T(8,128)S(1)}, f32[32,128]{1,0:T(8,128)S(1)}, bf16[256,1536]{1,0:T(8,128)(2,1)S(1)}, bf16[256,1536]{1,0:T(8,128)(2,1)S(1)}, f32[24,1536]{1,0:T(8,128)S(1)}) custom-call(f32[8,48,128]{2,1,0:T(8,128)S(1)} %all_to_all.15.spots_ref, f32[12,128]{1,0:T(8,128)S(1)} %get-tuple-element.17.charge_ref), custom_call_target="tpu_custom_call" | custom-call | tf_op jit(solution)/shard_map/structure/pallas_call | solution.py:478
  15.9 9.7 %all_to_all.16.partial_ref = f32[8,24,256]{2,1,0:T(8,128)S(1)} all-to-all(f32[8,24,256]{2,1,0:T(8,128)S(1)} %get-tuple-element.18), channel_id=1, replica_groups={{5,4,7,6,1,0,3,2},{21,20,23,22,17,16,19,18},{37,36,39,38,33,32,35,34},{..., dimensions={0} | all-to-all | bytes 393216 | tf_op jit(solution)/shard_map/all_to_all | solution.py:413
  25.6 0.5 %force.1 = f32[8,40,128]{2,1,0:T(8,128)S(1)} custom-call(f32[8,24,256]{2,1,0:T(8,128)S(1)} %all_to_all.16.partial_ref, f32[32,128]{1,0:T(8,128)S(1)} %get-tuple-element.19.weights_ref, bf16[256,1536]{1,0:T(8,128)(2,1)S(1)} %get-tuple-element.20.high_ref, bf16[256,1536]{1,0:T(8,128)(2,1)S(1)} %get-tuple-element.21.low_ref, ...), custom_call_target="tpu_custom_call" | custom-call | tf_op jit(solution)/shard_map/force/pallas_call | solution.py:494
  26.1 11.7 %all_to_all.17.force_ref = f32[8,40,128]{2,1,0:T(8,128)S(1)} all-to-all(f32[8,40,128]{2,1,0:T(8,128)S(1)} %force.1), channel_id=1, replica_groups={{88,72,120,104,16,0,48,32},{89,73,121,105,17,1,49,33},{90,74,122,106,18..., dimensions={0} | all-to-all | bytes 327680 | tf_op jit(solution)/shard_map/all_to_all | solution.py:413
  37.8 0.5 %collective-permute-start.1 = (f32[4,40,128]{2,1,0:T(8,128)S(1)}, f32[4,40,128]{2,1,0:T(8,128)S(1)}, u32[]{:S(2)}, u32[]{:S(2)}) collective-permute-start(f32[4,40,128]{2,1,0:T(8,128)S(1)} %gather.1.kept_ref), channel_id=1, source_target_pairs={{0,8},{8,0},{16,24},{24,16},{32,40},{40,32},{48,56},{56,48},{64,72... | collective-permute-start | bytes 245768 | tf_op jit(solution)/shard_map/ppermute | solution.py:420
  38.3 0.9 %collective-permute-done.1.taken_ref = f32[4,40,128]{2,1,0:T(8,128)S(1)} collective-permute-done((f32[4,40,128]{2,1,0:T(8,128)S(1)}, f32[4,40,128]{2,1,0:T(8,128)S(1)}, u32[]{:S(2)}, u32[]{:S(2)}) %collective-permute-start.1) | collective-permute-done | bytes 81952 | tf_op jit(solution)/shard_map/ppermute | solution.py:420
  39.2 0.7 %expand.1 = f32[3,8,1536]{2,1,0:T(8,128)} custom-call(f32[64,128]{1,0:T(8,128)S(1)} %get-tuple-element.14.table_ref, f32[8,40,128]{2,1,0:T(8,128)S(1)} %own.1.own_ref, f32[4,40,128]{2,1,0:T(8,128)S(1)} %collective-permute-done.1.taken_ref), custom_call_target="tpu_custom_call" | custom-call | tf_op jit(solution)/shard_map/expand/pallas_call | solution.py:524
  (3 shorter events, 0.1 us)
Async XLA Ops:
  1.0 2.4 %collective-permute-start = (f32[4,40,128]{2,1,0:T(8,128)S(1)}, f32[4,40,128]{2,1,0:T(8,128)S(1)}, u32[]{:S(2)}, u32[]{:S(2)}) collective-permute-start(f32[4,40,128]{2,1,0:T(8,128)S(1)} %get-tuple-element.16.given_ref), channel_id=1, source_target_pairs={{0,8},{8,0},{16,24},{24,16},{32,40},{40,32},{48,56},{56,48},{64,72... | collective-permute-start | bytes 245768 | tf_op jit(solution)/shard_map/ppermute | solution.py:420
  37.8 1.4 %collective-permute-start.1 = (f32[4,40,128]{2,1,0:T(8,128)S(1)}, f32[4,40,128]{2,1,0:T(8,128)S(1)}, u32[]{:S(2)}, u32[]{:S(2)}) collective-permute-start(f32[4,40,128]{2,1,0:T(8,128)S(1)} %gather.1.kept_ref), channel_id=1, source_target_pairs={{0,8},{8,0},{16,24},{24,16},{32,40},{40,32},{48,56},{56,48},{64,72... | collective-permute-start | bytes 245768 | tf_op jit(solution)/shard_map/ppermute | solution.py:420
